TPU v7x, 32 devices: a whole 2x2x4 slice. The times are simulated.
32 devices in a mesh: seq: 8 (over z, y), mp: 4 (over x, core).
Axes of the slice: x: 2, y: 2, z: 4, core: 2. Of those that a mesh axis runs over, the one named last changes fastest.
Arguments:
- y_first: bfloat16 [2048, 896], P('seq', 'mp'), may hold values from -6 to 6
- y_second: bfloat16 [2048, 896], P('seq', 'mp'), may hold values from -10 to 10
- grad_first: bfloat16 [2048, 896], P('seq', 'mp'), may hold values from -6 to 6
- grad_second: bfloat16 [2048, 896], P('seq', 'mp'), may hold values from -6 to 6
- doc_blocks: int32 [12], replicated, may hold values from 1 to 2, as said below
- last_fill: int32 [12], replicated, may hold values from 1 to 128
- plan: int32 [16], replicated, may hold values from 0 to 15, as said below
- q_weight: bfloat16 [896, 512], P(None, 'mp'), may hold values from -1 to 1
- kv_weight: bfloat16 [2, 896, 128], P(None, 'mp'), may hold values from -1 to 1
- out_weight: bfloat16 [512, 896], P('mp'), may hold values from -0.25 to 0.25
- gate_up: bfloat16 [2, 896, 2560], P(None, None, 'mp'), may hold values from -0.1875 to 0.1875
- down_weight: bfloat16 [2560, 896], P('mp'), may hold values from -0.125 to 0.125
Outputs:
- first_input: bfloat16 [2048, 896], P('seq', 'mp')
- second_input: bfloat16 [2048, 896], P('seq', 'mp')
- first_grad: bfloat16 [2048, 896], P('seq', 'mp')
- second_grad: bfloat16 [2048, 896], P('seq', 'mp')
- q_weight_grad: float32 [896, 512], P('seq', 'mp')
- kv_weight_grad: float32 [2, 896, 128], P(None, 'seq')
- out_weight_grad: float32 [512, 896], P('mp', 'seq')
Inputs may be any that keep to these rules, and one draw needn't show every extreme that they name: `doc_blocks`: each document holds 1 or 2 blocks; together they fill all 16 blocks; exactly 4 documents hold 2. A permutation: block b goes to slot plan[b]; slots k * 2 to (k + 1) * 2 - 1 belong to index k of seq; the blocks of one document go to consecutive slots of one index, in order, the first at an even slot.
All inputs are finite; a program needn't handle non-finite values.
Results may differ from a plain program's by a relative error of at most 0.024.
Values may be sent and summed in bfloat16 or wider, within the bound.
A program may use at most 64 MiB of HBM per device.

v0:
```python
import math

import jax
import jax.numpy as jnp
from jax import lax
from jax.sharding import PartitionSpec as P

BLOCK = 128


EPSILON = 1e-06


def for_sending(value):
    return jax.tree.map(lambda a: a.astype(jnp.bfloat16) if a.dtype == jnp.float32 else a, value)


def normalize(values):
    inverse = lax.rsqrt(jnp.mean(values * values, axis=-1, keepdims=True) + EPSILON)
    return (values * inverse, inverse)


def block_table(doc_blocks, last_fill, block_count):
    doc_count = doc_blocks.shape[0]
    starts = jnp.cumsum(doc_blocks) - doc_blocks
    index = jnp.arange(block_count, dtype=jnp.int32)
    owner_doc = jnp.sum((starts[None, :] <= index[:, None]).astype(jnp.int32), axis=1) - 1
    onehot = (owner_doc[:, None] == jnp.arange(doc_count, dtype=jnp.int32)[None, :]).astype(
        jnp.int32
    )
    first_block = jnp.sum(onehot * starts[None, :], axis=1)
    length = jnp.sum(onehot * doc_blocks[None, :], axis=1)
    filled = jnp.sum(onehot * last_fill[None, :], axis=1)
    limit = jnp.where(index - first_block == length - 1, filled, BLOCK)
    return (owner_doc, limit)


def attend_mask(doc_rows, valid_rows):
    count = doc_rows.shape[-1]
    order = jnp.arange(count, dtype=jnp.int32)
    causal = order[None, :] <= order[:, None]
    same_doc = doc_rows[..., :, None] == doc_rows[..., None, :]
    keep = valid_rows[..., None, :] | (order[None, :] == order[:, None])
    return same_doc & causal & keep


def contract_last(left, right):
    return lax.dot_general(
        left, right, (((1,), (1,)), ((), ())), preferred_element_type=jnp.float32
    )


def contract_first(left, right):
    return lax.dot_general(
        left, right, (((0,), (0,)), ((), ())), preferred_element_type=jnp.float32
    )


def to_owners(streams, source):
    pieces = lax.axis_size("seq")
    row_total, feat_width = streams[0].shape
    slot_count = row_total // BLOCK
    share_rows = BLOCK // pieces
    split = tuple((item.reshape(slot_count, pieces, share_rows, feat_width) for item in streams))
    held = jax.tree.map(
        lambda part, own: part.astype(own.dtype),
        lax.all_to_all(for_sending(split), "seq", split_axis=1, concat_axis=0, tiled=True),
        split,
    )
    placed = tuple(
        (item[source].reshape(pieces, slot_count, share_rows, feat_width) for item in held)
    )
    owned = jax.tree.map(
        lambda part, own: part.astype(own.dtype),
        lax.all_to_all(for_sending(placed), "seq", split_axis=0, concat_axis=2, tiled=True),
        placed,
    )
    return tuple((item.reshape(row_total, feat_width) for item in owned))


def shards(
    y_first,
    y_second,
    grad_first,
    grad_second,
    doc_blocks,
    last_fill,
    plan,
    q_weight,
    kv_weight,
    out_weight,
    gate_up,
    down_weight,
):
    f32 = jnp.float32
    bf16 = jnp.bfloat16
    block_count = plan.shape[0]
    source = (
        jnp.zeros((block_count,), jnp.int32).at[plan].set(jnp.arange(block_count, dtype=jnp.int32))
    )
    owner_doc, limit = block_table(doc_blocks, last_fill, block_count)
    moved = to_owners((y_first, y_second, grad_first, grad_second), source)
    share_width = moved[0].shape[1]
    first, second, cot_first, cot_second, kv_full = (
        lax.all_gather(moved[0], "mp", axis=1, tiled=True),
        lax.all_gather(moved[1], "mp", axis=1, tiled=True),
        lax.all_gather(moved[2], "mp", axis=1, tiled=True),
        lax.all_gather(moved[3], "mp", axis=1, tiled=True),
        lax.all_gather(kv_weight, "mp", axis=1, tiled=True),
    )
    row_total, width = first.shape
    slot_count = row_total // BLOCK
    owned_slots = lax.axis_index("seq") * slot_count + jnp.arange(slot_count, dtype=jnp.int32)
    mine = source[owned_slots]
    row_doc = jnp.repeat(owner_doc[mine], BLOCK, total_repeat_length=row_total)
    row_limit = jnp.repeat(limit[mine], BLOCK, total_repeat_length=row_total)
    valid = jnp.arange(row_total, dtype=jnp.int32) % BLOCK < row_limit
    column_start = lax.axis_index("mp") * share_width

    def own_share(values):
        return lax.dynamic_slice_in_dim(values, column_start, share_width, 1)

    n_one, r_one = normalize(first.astype(f32))
    n_one_b = n_one.astype(bf16)
    gate_pre = jnp.dot(n_one_b, gate_up[0], preferred_element_type=f32)
    up_pre = jnp.dot(n_one_b, gate_up[1], preferred_element_type=f32)
    sigma = jax.nn.sigmoid(gate_pre)
    silu_gate = gate_pre * sigma
    hidden = (silu_gate * up_pre).astype(bf16)
    mix_part = jnp.dot(hidden, down_weight, preferred_element_type=f32)
    mixed = lax.psum(mix_part, "mp")
    second_in = (second.astype(f32) - mixed).astype(bf16)
    d_hidden = contract_last(cot_second, down_weight)
    d_gate = (d_hidden * up_pre * sigma * (1.0 + gate_pre * (1.0 - sigma))).astype(bf16)
    d_up = (d_hidden * silu_gate).astype(bf16)
    norm_part = contract_last(d_gate, gate_up[0]) + contract_last(d_up, gate_up[1])
    norm_share = lax.psum_scatter(
        norm_part.astype(jnp.bfloat16), "mp", scatter_dimension=1, tiled=True
    ).astype(jnp.float32)
    n_one_share = own_share(n_one)
    inner = lax.psum(jnp.sum(norm_share * n_one_share, axis=1, keepdims=True), "mp") / width
    first_share = (moved[2].astype(f32) + (norm_share - n_one_share * inner) * r_one).astype(bf16)
    first_cot = lax.all_gather(first_share, "mp", axis=1, tiled=True)
    kv_count = kv_full.shape[0]
    head_size = kv_full.shape[2] // 2
    local_heads = q_weight.shape[1] // head_size
    per_group = local_heads * lax.axis_size("mp") // kv_count
    group = lax.axis_index("mp") * local_heads // per_group
    kv_local = lax.dynamic_index_in_dim(kv_full, group, 0, keepdims=False)
    n_two, r_two = normalize(second_in.astype(f32))
    n_two_b = n_two.astype(bf16)
    query = jnp.dot(n_two_b, q_weight, preferred_element_type=f32).astype(bf16)
    keyval = jnp.dot(n_two_b, kv_local, preferred_element_type=f32).astype(bf16)
    pair_rows = 2 * BLOCK
    pair_count = row_total // pair_rows
    query_groups = query.reshape(pair_count, pair_rows, local_heads, head_size)
    key_groups = keyval[:, :head_size].reshape(pair_count, pair_rows, head_size)
    value_groups = keyval[:, head_size:].reshape(pair_count, pair_rows, head_size)
    allowed = attend_mask(
        row_doc.reshape(pair_count, pair_rows), valid.reshape(pair_count, pair_rows)
    )
    scale = 1.0 / math.sqrt(head_size)
    scores = (
        jnp.einsum("gihd,gjd->ghij", query_groups, key_groups, preferred_element_type=f32) * scale
    )
    scores = jnp.where(allowed[:, None], scores, -1e30)
    highest = jnp.max(scores, axis=-1, keepdims=True)
    expo = jnp.exp(scores - highest)
    probs = expo / jnp.sum(expo, axis=-1, keepdims=True)
    probs_b = probs.astype(bf16)
    heads_out = (
        jnp.einsum("ghij,gjd->gihd", probs_b, value_groups, preferred_element_type=f32)
        .astype(bf16)
        .reshape(row_total, local_heads * head_size)
    )
    attn = lax.psum(
        jnp.dot(heads_out, out_weight, preferred_element_type=f32).astype(jnp.bfloat16), "mp"
    ).astype(jnp.float32)
    live = valid[:, None]
    first_in = (first.astype(f32) - live.astype(f32) * attn).astype(bf16)
    masked_cot = first_cot * live.astype(bf16)
    out_grad = contract_first(heads_out, masked_cot)
    d_out = (
        contract_last(masked_cot, out_weight)
        .astype(bf16)
        .reshape(pair_count, pair_rows, local_heads, head_size)
    )
    d_prob = jnp.einsum("gihd,gjd->ghij", d_out, value_groups, preferred_element_type=f32)
    delta = jnp.sum(probs * d_prob, axis=-1, keepdims=True)
    d_score = (probs * (d_prob - delta) * scale).astype(bf16)
    d_query = (
        jnp.einsum("ghij,gjd->gihd", d_score, key_groups, preferred_element_type=f32)
        .astype(bf16)
        .reshape(row_total, local_heads * head_size)
    )
    d_key = jnp.einsum("ghij,gihd->gjhd", d_score, query_groups, preferred_element_type=f32).astype(
        bf16
    )
    d_value = jnp.einsum("ghij,gihd->gjhd", probs_b, d_out, preferred_element_type=f32).astype(bf16)
    q_grad = contract_first(n_two_b, d_query)
    norm_groups = n_two_b.reshape(pair_count, pair_rows, width)
    key_grad = jnp.einsum("gsk,gshd->kd", norm_groups, d_key, preferred_element_type=f32)
    value_grad = jnp.einsum("gsk,gshd->kd", norm_groups, d_value, preferred_element_type=f32)
    kv_own = jnp.concatenate([key_grad, value_grad], axis=1)
    d_norm_two = contract_last(d_query, q_weight)
    d_norm_two = d_norm_two + jnp.einsum(
        "gshd,kd->gsk", d_key, kv_local[:, :head_size], preferred_element_type=f32
    ).reshape(row_total, width)
    d_norm_two = d_norm_two + jnp.einsum(
        "gshd,kd->gsk", d_value, kv_local[:, head_size:], preferred_element_type=f32
    ).reshape(row_total, width)
    d_norm_two = lax.psum(d_norm_two.astype(jnp.bfloat16), "mp").astype(jnp.float32)
    inner_two = jnp.mean(d_norm_two * n_two, axis=-1, keepdims=True)
    second_cot = (cot_second.astype(f32) + (d_norm_two - n_two * inner_two) * r_two).astype(bf16)
    q_share = lax.psum_scatter(q_grad, "seq", scatter_dimension=0, tiled=True)
    kv_grad = jnp.zeros((kv_count, width, 2 * head_size), f32)
    kv_grad = lax.dynamic_update_index_in_dim(kv_grad, kv_own, group, 0)
    out_share, kv_part = (
        lax.psum_scatter(out_grad, "seq", scatter_dimension=1, tiled=True),
        lax.psum_scatter(kv_grad, "seq", scatter_dimension=1, tiled=True),
    )
    kv_share = lax.psum(kv_part, "mp")
    return (
        own_share(first_in),
        own_share(second_in),
        first_share,
        own_share(second_cot),
        q_share,
        kv_share,
        out_share,
    )


def solution(mesh):
    return jax.shard_map(
        shards,
        mesh=mesh,
        in_specs=(
            P("seq", "mp"),
            P("seq", "mp"),
            P("seq", "mp"),
            P("seq", "mp"),
            P(),
            P(),
            P(),
            P(None, "mp"),
            P(None, "mp", None),
            P("mp", None),
            P(None, None, "mp"),
            P("mp", None),
        ),
        out_specs=(
            P("seq", "mp"),
            P("seq", "mp"),
            P("seq", "mp"),
            P("seq", "mp"),
            P("seq", "mp"),
            P(None, "seq", None),
            P("mp", "seq"),
        ),
        check_vma=False,
    )
```

profile of v0, /device:TPU:0, one launch (start us, length us, event | category | flops | bytes accessed | tf_op | source)
XLA Modules:
  0.0 467.6 jit_solution(3869260832934583238)
XLA Ops:
  7.2 1.1 copy.93
  9.0 7.3 %all-to-all-start = ((bf16[2,8,16,224]{3,2,0,1:T(8,128)(2,1)}), bf16[2,8,16,224]{3,2,0,1:T(8,128)(2,1)S(1)}, u32[]{:S(2)}, u32[]{:S(2)}) async-start(bf16[2,8,16,224]{3,2,0,1:T(8,128)(2,1)} %copy.94), calls=%async_computation | async-start | bytes 262144 | tf_op jit(solution)/shard_map/all_to_all | solution.py:67
  23.6 5.5 %all-to-all-start.6 = ((bf16[2,8,16,224]{3,2,0,1:T(8,128)(2,1)}), bf16[2,8,16,224]{3,2,0,1:T(8,128)(2,1)S(1)}, u32[]{:S(2)}, u32[]{:S(2)}) async-start(bf16[2,8,16,224]{3,2,0,1:T(8,128)(2,1)} %copy.107), calls=%async_computation.6 | async-start | bytes 262144 | tf_op jit(solution)/shard_map/all_to_all | solution.py:67
  29.7 6.8 %all-to-all-done.6 = bf16[2,8,16,224]{3,2,0,1:T(8,128)(2,1)S(1)} async-done(((bf16[2,8,16,224]{3,2,0,1:T(8,128)(2,1)}), bf16[2,8,16,224]{3,2,0,1:T(8,128)(2,1)S(1)}, u32[]{:S(2)}, u32[]{:S(2)}) %all-to-all-start.6) | async-done | bytes 114720 | tf_op jit(solution)/shard_map/all_to_all | solution.py:67
  36.5 3.4 all-to-all-start.4
  39.8 1.3 fusion.71
  42.0 6.8 %all_gather.17 = bf16[2,896,128]{2,1,0:T(8,128)(2,1)S(1)} all-gather(bf16[2,224,128]{2,1,0:T(8,128)(2,1)S(1)} %copy-done.16), channel_id=1, replica_groups=mesh['seq'=8,'mp'=4] {'mp'}, dimensions={1}, use_global_device_ids=true | all-gather | bytes 573440 | tf_op jit(solution)/shard_map/all_gather | solution.py:109
  48.8 5.9 %all-to-all-start.2 = ((bf16[2,8,16,224]{3,2,0,1:T(8,128)(2,1)}), bf16[2,8,16,224]{3,2,0,1:T(8,128)(2,1)S(1)}, u32[]{:S(2)}, u32[]{:S(2)}) async-start(bf16[2,8,16,224]{3,2,0,1:T(8,128)(2,1)} %copy.98), calls=%async_computation.2 | async-start | bytes 262144 | tf_op jit(solution)/shard_map/all_to_all | solution.py:67
  54.7 1.3 select_select_fusion
  56.0 1.2 gather_fusion
  57.2 5.0 %all-to-all-done.2 = bf16[2,8,16,224]{3,2,0,1:T(8,128)(2,1)S(1)} async-done(((bf16[2,8,16,224]{3,2,0,1:T(8,128)(2,1)}), bf16[2,8,16,224]{3,2,0,1:T(8,128)(2,1)S(1)}, u32[]{:S(2)}, u32[]{:S(2)}) %all-to-all-start.2) | async-done | bytes 114720 | tf_op jit(solution)/shard_map/all_to_all | solution.py:67
  62.2 3.4 all-to-all-start.1
  66.3 1.2 gather_fusion.6
  67.5 1.2 gather_fusion.5
  68.7 1.2 gather_fusion.3
  69.9 2.9 all-to-all-done.1
  72.8 3.4 all-to-all-start.7
  76.4 6.3 %all_gather.15 = bf16[256,896]{0,1:T(8,128)(2,1)S(1)} all-gather(bf16[256,224]{0,1:T(8,128)(2,1)S(1)} %copy.96), channel_id=1, replica_groups=mesh['seq'=8,'mp'=4] {'mp'}, dimensions={1}, use_global_device_ids=true | all-gather | bytes 573440 | tf_op jit(solution)/shard_map/all_gather | solution.py:105
  82.8 2.8 fusion.9
  85.7 1.4 fusion.5
  87.1 5.9 %all-to-all-start.5 = ((bf16[8,2,16,224]{3,2,1,0:T(8,128)(2,1)}), bf16[8,2,16,224]{3,2,1,0:T(8,128)(2,1)S(1)}, u32[]{:S(2)}, u32[]{:S(2)}) async-start(bf16[8,2,16,224]{3,2,1,0:T(8,128)(2,1)} %bitcast.42), calls=%async_computation.5 | async-start | bytes 262144 | tf_op jit(solution)/shard_map/all_to_all | solution.py:75
  93.2 6.8 %all_gather.18 = bf16[256,896]{0,1:T(8,128)(2,1)S(1)} all-gather(bf16[256,224]{0,1:T(8,128)(2,1)S(1)} %copy.109), channel_id=1, replica_groups=mesh['seq'=8,'mp'=4] {'mp'}, dimensions={1}, use_global_device_ids=true | all-gather | bytes 573440 | tf_op jit(solution)/shard_map/all_gather | solution.py:108
  100.6 3.2 fusion.7
  103.8 1.5 fusion.26
  105.4 5.7 %all-to-all-start.3 = ((bf16[8,2,16,224]{3,2,1,0:T(8,128)(2,1)}), bf16[8,2,16,224]{3,2,1,0:T(8,128)(2,1)S(1)}, u32[]{:S(2)}, u32[]{:S(2)}) async-start(bf16[8,2,16,224]{3,2,1,0:T(8,128)(2,1)} %bitcast.20), calls=%async_computation.3 | async-start | bytes 262144 | tf_op jit(solution)/shard_map/all_to_all | solution.py:75
  112.9 5.7 %all-to-all-done.3 = bf16[8,2,16,224]{3,2,1,0:T(8,128)(2,1)S(1)} async-done(((bf16[8,2,16,224]{3,2,1,0:T(8,128)(2,1)}), bf16[8,2,16,224]{3,2,1,0:T(8,128)(2,1)S(1)}, u32[]{:S(2)}, u32[]{:S(2)}) %all-to-all-start.3) | async-done | bytes 114720 | tf_op jit(solution)/shard_map/all_to_all | solution.py:75
  118.7 8.9 %all_gather.16 = bf16[256,896]{0,1:T(8,128)(2,1)S(1)} all-gather(bf16[256,224]{0,1:T(8,128)(2,1)S(1)} %copy.100), channel_id=1, replica_groups=mesh['seq'=8,'mp'=4] {'mp'}, dimensions={1}, use_global_device_ids=true | all-gather | bytes 573440 | tf_op jit(solution)/shard_map/all_gather | solution.py:106
  127.8 3.4 fusion.1
  131.3 19.7 %all-reduce.5.cloned.1.call-done = f32[256,896]{1,0:T(8,128)} async-done(((f32[256,896]{1,0:T(8,128)}), f32[256,896]{1,0:T(8,128)}) %all-reduce.5.cloned.1.call-update) | async-done | bytes 917520 | tf_op jit(solution)/shard_map/psum | solution.py:131
  150.9 1.4 fusion.19
  152.8 1.3 convolution_convert_fusion.2
  155.8 1.1 convolution_convert_fusion
  156.9 17.9 %reduce-scatter.5.cloned.1.call-done = bf16[256,224]{0,1:T(8,128)(2,1)} async-done(((bf16[256,896]{0,1:T(8,128)(2,1)}), bf16[256,224]{0,1:T(8,128)(2,1)}) %reduce-scatter.5.cloned.1.call-update) | async-done | bytes 114704 | tf_op jit(solution)/shard_map/reduce_scatter | solution.py:137
  174.9 1.0 fusion.37
  175.9 5.8 %psum.37 = f32[256,1]{0,1:T(1,128)S(1)} all-reduce(f32[256,1]{0,1:T(1,128)S(1)} %bitcast.175), channel_id=1, replica_groups=mesh['seq'=8,'mp'=4] {'mp'}, use_global_device_ids=true, to_apply=%region_14.16 | all-reduce | flops 256 | bytes 2048 | tf_op jit(solution)/shard_map/psum | solution.py:141
  181.7 1.1 fusion.40
  182.8 6.5 %all_gather.19 = bf16[256,896]{0,1:T(8,128)(2,1)S(1)} all-gather(bf16[256,224]{0,1:T(8,128)(2,1)S(1)} %fusion.40), channel_id=1, replica_groups=mesh['seq'=8,'mp'=4] {'mp'}, dimensions={1}, use_global_device_ids=true | all-gather | bytes 573440 | tf_op jit(solution)/shard_map/all_gather | solution.py:143
  192.2 1.2 fusion
  196.9 2.1 fusion.23
  199.8 1.2 fusion.67
  202.1 27.5 %all-reduce.9.cloned.1.call-done = (bf16[256,896]{0,1:T(8,128)(2,1)}, bf16[256,896]{1,0:T(8,128)(2,1)}) async-done(((bf16[256,896]{0,1:T(8,128)(2,1)}, bf16[256,896]{1,0:T(8,128)(2,1)}), (bf16[256,896]{0,1:T(8,128)(2,1)}, bf16[256,896]{1,0:T(8,128)(2,1)})) %all-reduce.9.cloned.1.call-update) | async-done | bytes 917520 | tf_op jit(solution)/shard_map/psum | solution.py:176
  229.6 1.2 convert_element_type.176
  231.4 65.5 %reduce-scatter.9.cloned.1.call-done = f32[2,112,128]{2,1,0:T(8,128)} async-done(((f32[2,896,128]{2,1,0:T(8,128)}), f32[2,112,128]{2,1,0:T(8,128)}) %reduce-scatter.9.cloned.1.call-update) | async-done | bytes 114704 | tf_op jit(solution)/shard_map/reduce_scatter | solution.py:220
  296.9 1.6 fusion.43
  299.3 62.8 %reduce-scatter.11.cloned.1.call-done = f32[128,112]{0,1:T(8,128)} async-done(((f32[128,896]{0,1:T(8,128)}), f32[128,112]{0,1:T(8,128)}) %reduce-scatter.11.cloned.1.call-update) | async-done | bytes 57360 | tf_op jit(solution)/shard_map/reduce_scatter | solution.py:219
  362.1 65.3 %reduce-scatter.7.cloned.1.call-done = f32[112,128]{1,0:T(8,128)} async-done(((f32[896,128]{1,0:T(8,128)}), f32[112,128]{1,0:T(8,128)}) %reduce-scatter.7.cloned.1.call-update) | async-done | bytes 57360 | tf_op jit(solution)/shard_map/reduce_scatter | solution.py:215
  427.4 31.8 %all-reduce.7.cloned.1.call-done = f32[2,112,128]{2,1,0:T(8,128)} async-done(((f32[2,112,128]{2,1,0:T(8,128)}), f32[2,112,128]{2,1,0:T(8,128)}) %all-reduce.7.cloned.1.call-update) | async-done | bytes 114704 | tf_op jit(solution)/shard_map/psum | solution.py:222
  459.2 1.6 copy.128
  (151 shorter events, 24.8 us)
Async XLA Ops:
  7.2 92.8 %copy-start = (bf16[640,896]{1,0:T(8,128)(2,1)S(1)}, bf16[640,896]{1,0:T(8,128)(2,1)}, u32[]{:S(2)}) copy-start(bf16[640,896]{1,0:T(8,128)(2,1)} %param.29) | copy-start | bytes 3440644
  7.2 11.4 %copy-start.14 = (bf16[256,224]{0,1:T(8,128)(2,1)S(1)}, bf16[256,224]{0,1:T(8,128)(2,1)}, u32[]{:S(2)}) copy-start(bf16[256,224]{0,1:T(8,128)(2,1)} %param.20) | copy-start | bytes 344068
  7.2 12.2 %copy-start.24 = (s32[12]{0:T(128)S(1)}, s32[12]{0:T(128)}, u32[]{:S(2)}) copy-start(s32[12]{0:T(128)} %param.22) | copy-start | bytes 148
  7.2 13.8 %copy-start.25 = (s32[12]{0:T(128)S(1)}, s32[12]{0:T(128)}, u32[]{:S(2)}) copy-start(s32[12]{0:T(128)} %param.23) | copy-start | bytes 148
  9.0 14.7 %all-to-all-start = ((bf16[2,8,16,224]{3,2,0,1:T(8,128)(2,1)}), bf16[2,8,16,224]{3,2,0,1:T(8,128)(2,1)S(1)}, u32[]{:S(2)}, u32[]{:S(2)}) async-start(bf16[2,8,16,224]{3,2,0,1:T(8,128)(2,1)} %copy.94), calls=%async_computation | async-start | bytes 262144 | tf_op jit(solution)/shard_map/all_to_all | solution.py:67
  19.4 21.8 %copy-start.15 = (bf16[256,224]{0,1:T(8,128)(2,1)S(1)}, bf16[256,224]{0,1:T(8,128)(2,1)}, u32[]{:S(2)}) copy-start(bf16[256,224]{0,1:T(8,128)(2,1)} %param.19) | copy-start | bytes 344068
  21.0 21.0 %copy-start.16 = (bf16[2,224,128]{2,1,0:T(8,128)(2,1)S(1)}, bf16[2,224,128]{2,1,0:T(8,128)(2,1)}, u32[]{:S(2)}) copy-start(bf16[2,224,128]{2,1,0:T(8,128)(2,1)} %param.26) | copy-start | bytes 344068
  23.6 12.8 %all-to-all-start.6 = ((bf16[2,8,16,224]{3,2,0,1:T(8,128)(2,1)}), bf16[2,8,16,224]{3,2,0,1:T(8,128)(2,1)S(1)}, u32[]{:S(2)}, u32[]{:S(2)}) async-start(bf16[2,8,16,224]{3,2,0,1:T(8,128)(2,1)} %copy.107), calls=%async_computation.6 | async-start | bytes 262144 | tf_op jit(solution)/shard_map/all_to_all | solution.py:67
  36.5 12.3 %all-to-all-start.4 = ((bf16[2,8,16,224]{3,2,0,1:T(8,128)(2,1)}), bf16[2,8,16,224]{3,2,0,1:T(8,128)(2,1)S(1)}, u32[]{:S(2)}, u32[]{:S(2)}) async-start(bf16[2,8,16,224]{3,2,0,1:T(8,128)(2,1)} %copy.104), calls=%async_computation.4 | async-start | bytes 262144 | tf_op jit(solution)/shard_map/all_to_all | solution.py:67
  41.1 24.4 %copy-start.22 = (pred[256]{0:T(512)(128)(4,1)}, pred[256]{0:T(512)(128)(4,1)S(1)}, u32[]{:S(2)}) copy-start(pred[256]{0:T(512)(128)(4,1)S(1)} %get-tuple-element.69) | copy-start | bytes 772
  48.8 13.4 %all-to-all-start.2 = ((bf16[2,8,16,224]{3,2,0,1:T(8,128)(2,1)}), bf16[2,8,16,224]{3,2,0,1:T(8,128)(2,1)S(1)}, u32[]{:S(2)}, u32[]{:S(2)}) async-start(bf16[2,8,16,224]{3,2,0,1:T(8,128)(2,1)} %copy.98), calls=%async_computation.2 | async-start | bytes 262144 | tf_op jit(solution)/shard_map/all_to_all | solution.py:67
  62.2 10.7 %all-to-all-start.1 = ((bf16[8,2,16,224]{3,2,1,0:T(8,128)(2,1)}), bf16[8,2,16,224]{3,2,1,0:T(8,128)(2,1)S(1)}, u32[]{:S(2)}, u32[]{:S(2)}) async-start(bf16[8,2,16,224]{3,2,1,0:T(8,128)(2,1)} %bitcast.4), calls=%async_computation.1 | async-start | bytes 262144 | tf_op jit(solution)/shard_map/all_to_all | solution.py:75
  72.8 14.3 %all-to-all-start.7 = ((bf16[8,2,16,224]{3,2,1,0:T(8,128)(2,1)}), bf16[8,2,16,224]{3,2,1,0:T(8,128)(2,1)S(1)}, u32[]{:S(2)}, u32[]{:S(2)}) async-start(bf16[8,2,16,224]{3,2,1,0:T(8,128)(2,1)} %bitcast.50), calls=%async_computation.7 | async-start | bytes 262144 | tf_op jit(solution)/shard_map/all_to_all | solution.py:75
  82.8 2.8 copy-start.26
  87.1 18.2 %all-to-all-start.5 = ((bf16[8,2,16,224]{3,2,1,0:T(8,128)(2,1)}), bf16[8,2,16,224]{3,2,1,0:T(8,128)(2,1)S(1)}, u32[]{:S(2)}, u32[]{:S(2)}) async-start(bf16[8,2,16,224]{3,2,1,0:T(8,128)(2,1)} %bitcast.42), calls=%async_computation.5 | async-start | bytes 262144 | tf_op jit(solution)/shard_map/all_to_all | solution.py:75
  93.2 7.4 %copy-start.27 = (bf16[2,896,640]{2,1,0:T(8,128)(2,1)S(1)}, bf16[2,896,640]{2,1,0:T(8,128)(2,1)}, u32[]{:S(2)}) copy-start(bf16[2,896,640]{2,1,0:T(8,128)(2,1)} %param.28) | copy-start | bytes 6881284
  100.6 4.8 %copy-start.5 = (f32[256,640]{1,0:T(8,128)}, f32[256,640]{1,0:T(8,128)S(1)}, u32[]{:S(2)}) copy-start(f32[256,640]{1,0:T(8,128)S(1)} %fusion.76) | copy-start | bytes 1966084
  100.6 3.2 copy-start.28
  100.6 3.2 copy-start.29
  105.4 13.2 %all-to-all-start.3 = ((bf16[8,2,16,224]{3,2,1,0:T(8,128)(2,1)}), bf16[8,2,16,224]{3,2,1,0:T(8,128)(2,1)S(1)}, u32[]{:S(2)}, u32[]{:S(2)}) async-start(bf16[8,2,16,224]{3,2,1,0:T(8,128)(2,1)} %bitcast.20), calls=%async_computation.3 | async-start | bytes 262144 | tf_op jit(solution)/shard_map/all_to_all | solution.py:75
  111.1 39.9 %all-reduce.5.cloned.1.call-start = ((), (), s32[]{:S(2)}) async-start(), calls=%async_computation.12 | async-start | bytes 1835008 | tf_op jit(solution)/shard_map/psum | solution.py:131
  111.8 63.0 %reduce-scatter.5.cloned.1.call-start = ((), (), s32[]{:S(2)}) async-start(), calls=%async_computation.13 | async-start | bytes 573440 | tf_op jit(solution)/shard_map/reduce_scatter | solution.py:137
  131.2 98.4 %all-reduce.9.cloned.1.call-start = ((), (), s32[]{:S(2)}) async-start(), calls=%async_computation.18 | async-start | bytes 1835008 | tf_op jit(solution)/shard_map/psum | solution.py:176
  152.3 1.8 copy-start.17
  152.8 2.3 copy-start.20
  154.1 0.6 copy-start.18
  154.9 0.9 copy-start.12
  155.1 0.6 copy-start.9
  181.7 7.6 %copy-start.13 = (bf16[128,896]{1,0:T(8,128)(2,1)S(1)}, bf16[128,896]{1,0:T(8,128)(2,1)}, u32[]{:S(2)}) copy-start(bf16[128,896]{1,0:T(8,128)(2,1)} %param.27) | copy-start | bytes 688132
  181.7 7.9 %copy-start.21 = (bf16[256,128]{0,1:T(8,128)(2,1)S(1)}, bf16[256,128]{0,1:T(8,128)(2,1)}, u32[]{:S(2)}) copy-start(bf16[256,128]{0,1:T(8,128)(2,1)} %copy-done.20) | copy-start | bytes 196612
  182.8 7.0 %copy-start.8 = (bf16[256,224]{0,1:T(8,128)(2,1)}, bf16[256,224]{0,1:T(8,128)(2,1)S(1)}, u32[]{:S(2)}) copy-start(bf16[256,224]{0,1:T(8,128)(2,1)S(1)} %fusion.40) | copy-start | bytes 344068
  189.3 0.8 copy-start.3
  190.0 0.8 copy-start.19
  190.1 1.5 copy-start.11
  191.3 1.0 copy-start.6
  193.4 103.5 %reduce-scatter.9.cloned.1.call-start = ((), (), s32[]{:S(2)}) async-start(), calls=%async_computation.15 | async-start | bytes 1032192 | tf_op jit(solution)/shard_map/reduce_scatter | solution.py:220
  194.8 1.0 copy-start.2
  195.8 1.1 copy-start.10
  195.8 0.9 copy-start.1
  195.9 3.2 copy-start.23
  196.8 165.3 %reduce-scatter.11.cloned.1.call-start = ((), (), s32[]{:S(2)}) async-start(), calls=%async_computation.17 | async-start | bytes 516096 | tf_op jit(solution)/shard_map/reduce_scatter | solution.py:219
  198.9 0.8 copy-start.7
  199.0 228.4 %reduce-scatter.7.cloned.1.call-start = ((), (), s32[]{:S(2)}) async-start(), calls=%async_computation.14 | async-start | bytes 516096 | tf_op jit(solution)/shard_map/reduce_scatter | solution.py:215
  201.0 258.1 %all-reduce.7.cloned.1.call-start = ((), (), s32[]{:S(2)}) async-start(), calls=%async_computation.16 | async-start | bytes 229376 | tf_op jit(solution)/shard_map/psum | solution.py:222
  229.6 1.2 copy-start.4
Sparse Core Ops, SparseCore 0:
  114.3 36.6 all-reduce.4
  153.5 21.3 reduce-scatter.4
  193.5 36.0 all-reduce.8
  232.8 64.0 reduce-scatter.8
  300.6 61.4 reduce-scatter.10
  365.8 61.5 reduce-scatter.6
  429.7 29.4 all-reduce.6
where the time goes:
time: 469 us; the launch traced here: 468 us
  waiting for transfers between devices  312 us (67%)
  blocking collectives  41 us (9%)
  starting transfers between devices  40.8 us (9%)
  matrix products  23.1 us (5%)
  local copies, waits for them, and re-layouts  22.9 us (5%)
  between operations  14.8 us (3%)
  other arithmetic  13 us (3%)
    reduce_scatter x1, waiting for transfers between devices, shards(): lax.psum_scatter(kv_grad, 'seq', scatter_dimension=1, tiled=True)  65.5 us
    reduce_scatter x1, waiting for transfers between devices, shards(): q_share = lax.psum_scatter(q_grad, 'seq', scatter_dimension=0, tiled=True)  65.3 us
    reduce_scatter x1, waiting for transfers between devices, shards(): lax.psum_scatter(out_grad, 'seq', scatter_dimension=1, tiled=True)  62.8 us
    psum x1, waiting for transfers between devices, shards(): kv_share = lax.psum(kv_part, 'mp')  31.8 us
    psum x1, waiting for transfers between devices, shards(): lax.psum(jnp.dot(heads_out, out_weight, preferred_element_type=f32).astyp...  27.5 us
    all_to_all x4, starting transfers between devices, to_owners(): lax.all_to_all(for_sending(split), 'seq', split_axis=1, concat_axis=0, ti...  22.1 us
    psum x1, waiting for transfers between devices, shards(): mixed = lax.psum(mix_part, 'mp')  19.7 us
    all_to_all x4, starting transfers between devices, to_owners(): lax.all_to_all(for_sending(placed), 'seq', split_axis=0, concat_axis=2, t...  18.4 us
  transfers between devices with their start and end apart: 15, of which 12 were waited for; matrix products, arithmetic and copies ran while one was open for 10% of the time, Pallas kernels for 0%

commit v1 on v0

v1 whole, which is shorter than its diff:
```python
import functools
import math

import jax
import jax.numpy as jnp
from jax import lax
from jax.experimental import pallas as pl
from jax.experimental.pallas import tpu as pltpu
from jax.sharding import PartitionSpec as P

BLOCK = 128


EPSILON = 1e-06


def each(start, stop, body):
    if stop - start <= 8:
        for k in range(start, stop):
            body(k)
    else:
        lax.fori_loop(start, stop, lambda k, c: (body(k), c)[1], 0)


def exchange_kernel(plans, *refs):
    count = len(plans)
    sources, targets = refs[:count], refs[count : 2 * count]
    send_sems = refs[2 * count : 3 * count]
    recv_sems = refs[3 * count : 4 * count]
    own_sem = refs[4 * count]
    barrier = pltpu.get_barrier_semaphore()
    sizes = dict((axis, size) for axis, size, _ in plans)
    for axis, size in sizes.items():
        me = lax.axis_index(axis)

        def greet(k):
            pl.semaphore_signal(
                barrier,
                inc=1,
                device_id={axis: lax.rem(me + k, size)},
                device_id_type=pl.DeviceIdType.MESH,
            )

        each(1, size, greet)
    pl.semaphore_wait(barrier, sum(size - 1 for size in sizes.values()))

    def copy_of(i, k):
        axis, size, gather = plans[i]
        me = lax.axis_index(axis)
        peer = lax.rem(me + k, size)
        return pltpu.make_async_remote_copy(
            src_ref=sources[i] if gather else sources[i].at[peer],
            dst_ref=targets[i].at[me],
            send_sem=send_sems[i].at[k],
            recv_sem=recv_sems[i].at[k],
            device_id={axis: peer},
            device_id_type=pl.DeviceIdType.MESH,
        )

    def own_copy(i):
        axis, _, gather = plans[i]
        me = lax.axis_index(axis)
        source = sources[i] if gather else sources[i].at[me]
        return pltpu.make_async_copy(source, targets[i].at[me], own_sem.at[i])

    for i in range(count):
        each(1, plans[i][1], lambda k: copy_of(i, k).start())
        own_copy(i).start()
    for i in range(count):
        each(1, plans[i][1], lambda k: copy_of(i, k).wait())
        own_copy(i).wait()


def exchange(number, *items):
    plans = tuple((axis, lax.axis_size(axis), gather) for _, axis, gather in items)
    arrays = [array for array, _, _ in items]
    shapes = [
        jax.ShapeDtypeStruct((size,) + (a.shape if gather else a.shape[1:]), a.dtype)
        for a, (_, size, gather) in zip(arrays, plans)
    ]
    sems = [pltpu.SemaphoreType.DMA((size,)) for _, size, _ in plans]
    return pl.pallas_call(
        functools.partial(exchange_kernel, plans),
        out_shape=shapes,
        in_specs=[pl.BlockSpec(memory_space=pl.ANY)] * len(arrays),
        out_specs=[pl.BlockSpec(memory_space=pl.ANY)] * len(arrays),
        scratch_shapes=sems + sems + [pltpu.SemaphoreType.DMA((len(arrays),))],
        compiler_params=pltpu.CompilerParams(collective_id=number, has_side_effects=True),
    )(*arrays)


def normalize(values):
    inverse = lax.rsqrt(jnp.mean(values * values, axis=-1, keepdims=True) + EPSILON)
    return (values * inverse, inverse)


def block_table(doc_blocks, last_fill, block_count):
    doc_count = doc_blocks.shape[0]
    starts = jnp.cumsum(doc_blocks) - doc_blocks
    index = jnp.arange(block_count, dtype=jnp.int32)
    owner_doc = jnp.sum((starts[None, :] <= index[:, None]).astype(jnp.int32), axis=1) - 1
    onehot = (owner_doc[:, None] == jnp.arange(doc_count, dtype=jnp.int32)[None, :]).astype(
        jnp.int32
    )
    first_block = jnp.sum(onehot * starts[None, :], axis=1)
    length = jnp.sum(onehot * doc_blocks[None, :], axis=1)
    filled = jnp.sum(onehot * last_fill[None, :], axis=1)
    limit = jnp.where(index - first_block == length - 1, filled, BLOCK)
    return (owner_doc, limit)


def attend_mask(doc_rows, valid_rows):
    count = doc_rows.shape[-1]
    order = jnp.arange(count, dtype=jnp.int32)
    causal = order[None, :] <= order[:, None]
    same_doc = doc_rows[..., :, None] == doc_rows[..., None, :]
    keep = valid_rows[..., None, :] | (order[None, :] == order[:, None])
    return same_doc & causal & keep


def contract_last(left, right):
    return lax.dot_general(
        left, right, (((1,), (1,)), ((), ())), preferred_element_type=jnp.float32
    )


def contract_first(left, right):
    return lax.dot_general(
        left, right, (((0,), (0,)), ((), ())), preferred_element_type=jnp.float32
    )


def to_chunks(values, pieces):
    rows, width = values.shape
    return values.reshape(rows, pieces, width // pieces).transpose(1, 0, 2)


def from_chunks(values):
    pieces, rows, width = values.shape
    return values.transpose(1, 0, 2).reshape(rows, pieces * width)


def total(values):
    return jnp.sum(values.astype(jnp.float32), axis=0)


def shards(
    y_first,
    y_second,
    grad_first,
    grad_second,
    doc_blocks,
    last_fill,
    plan,
    q_weight,
    kv_weight,
    out_weight,
    gate_up,
    down_weight,
):
    f32 = jnp.float32
    bf16 = jnp.bfloat16
    block_count = plan.shape[0]
    seq_size = lax.axis_size("seq")
    mp_size = lax.axis_size("mp")
    order = jnp.arange(block_count, dtype=jnp.int32)
    source = jnp.sum(jnp.where(plan[None, :] == order[:, None], order[None, :], 0), axis=1)
    owner_doc, limit = block_table(doc_blocks, last_fill, block_count)

    row_total, share_width = y_first.shape
    width = share_width * mp_size
    slot_count = row_total // BLOCK
    share_rows = BLOCK // seq_size
    kv_count = kv_weight.shape[0]
    head_size = kv_weight.shape[2] // 2
    local_heads = q_weight.shape[1] // head_size
    per_group = local_heads * mp_size // kv_count
    group_of = [p * local_heads // per_group for p in range(mp_size)]

    streams = jnp.stack(
        [
            item.reshape(slot_count, seq_size, share_rows, share_width).transpose(1, 0, 2, 3)
            for item in (y_first, y_second, grad_first, grad_second)
        ],
        axis=1,
    )
    kv_sent = jnp.stack([kv_weight[g] for g in group_of])
    held, kv_parts = exchange(0, (streams, "seq", False), (kv_sent, "mp", False))
    kv_local = kv_parts.reshape(width, 2 * head_size)
    placed = held[source // slot_count, :, source % slot_count]
    placed = placed.reshape(seq_size, slot_count, 4, share_rows, share_width)
    (owned,) = exchange(1, (placed, "seq", False))
    moved = owned.transpose(2, 1, 0, 3, 4).reshape(4, row_total, share_width)
    gathered = exchange(2, (moved[0], "mp", True), (moved[3], "mp", True))
    first, cot_second = (from_chunks(item) for item in gathered)

    owned_slots = lax.axis_index("seq") * slot_count + jnp.arange(slot_count, dtype=jnp.int32)
    mine = source[owned_slots]
    row_doc = jnp.repeat(owner_doc[mine], BLOCK, total_repeat_length=row_total)
    row_limit = jnp.repeat(limit[mine], BLOCK, total_repeat_length=row_total)
    valid = jnp.arange(row_total, dtype=jnp.int32) % BLOCK < row_limit

    n_one, r_one = normalize(first.astype(f32))
    n_one_b = n_one.astype(bf16)
    gate_pre = jnp.dot(n_one_b, gate_up[0], preferred_element_type=f32)
    up_pre = jnp.dot(n_one_b, gate_up[1], preferred_element_type=f32)
    sigma = jax.nn.sigmoid(gate_pre)
    silu_gate = gate_pre * sigma
    hidden = (silu_gate * up_pre).astype(bf16)
    mix_part = jnp.dot(hidden, down_weight, preferred_element_type=f32).astype(bf16)
    d_hidden = contract_last(cot_second, down_weight)
    d_gate = (d_hidden * up_pre * sigma * (1.0 + gate_pre * (1.0 - sigma))).astype(bf16)
    d_up = (d_hidden * silu_gate).astype(bf16)
    norm_part = contract_last(d_gate, gate_up[0]) + contract_last(d_up, gate_up[1])
    inner_part = jnp.sum(d_gate.astype(f32) * gate_pre + d_up.astype(f32) * up_pre, axis=1)
    mix_got, norm_got, inner_got = exchange(
        3,
        (to_chunks(mix_part, mp_size), "mp", False),
        (to_chunks(norm_part.astype(bf16), mp_size), "mp", False),
        (inner_part.reshape(slot_count, BLOCK), "mp", True),
    )
    second_share = (moved[1].astype(f32) - total(mix_got)).astype(bf16)
    inner = (total(inner_got) / width).reshape(row_total, 1)
    n_one_share = moved[0].astype(f32) * r_one
    first_share = (
        moved[2].astype(f32) + (total(norm_got) - n_one_share * inner) * r_one
    ).astype(bf16)
    second_all, cot_all = exchange(4, (second_share, "mp", True), (first_share, "mp", True))
    second_in = from_chunks(second_all)
    first_cot = from_chunks(cot_all)

    n_two, r_two = normalize(second_in.astype(f32))
    n_two_b = n_two.astype(bf16)
    query_full = jnp.dot(n_two_b, q_weight, preferred_element_type=f32)
    keyval_full = jnp.dot(n_two_b, kv_local, preferred_element_type=f32)
    query = query_full.astype(bf16)
    keyval = keyval_full.astype(bf16)
    pair_rows = 2 * BLOCK
    pair_count = row_total // pair_rows
    query_groups = query.reshape(pair_count, pair_rows, local_heads, head_size)
    key_groups = keyval[:, :head_size].reshape(pair_count, pair_rows, head_size)
    value_groups = keyval[:, head_size:].reshape(pair_count, pair_rows, head_size)
    allowed = attend_mask(
        row_doc.reshape(pair_count, pair_rows), valid.reshape(pair_count, pair_rows)
    )
    scale = 1.0 / math.sqrt(head_size)
    scores = (
        jnp.einsum("gihd,gjd->ghij", query_groups, key_groups, preferred_element_type=f32) * scale
    )
    scores = jnp.where(allowed[:, None], scores, -1e30)
    highest = jnp.max(scores, axis=-1, keepdims=True)
    expo = jnp.exp(scores - highest)
    probs = expo / jnp.sum(expo, axis=-1, keepdims=True)
    probs_b = probs.astype(bf16)
    heads_out = (
        jnp.einsum("ghij,gjd->gihd", probs_b, value_groups, preferred_element_type=f32)
        .astype(bf16)
        .reshape(row_total, local_heads * head_size)
    )
    attn_part = jnp.dot(heads_out, out_weight, preferred_element_type=f32).astype(bf16)
    live = valid[:, None]
    masked_cot = first_cot * live.astype(bf16)
    out_grad = contract_first(masked_cot, heads_out)
    d_out = (
        contract_last(masked_cot, out_weight)
        .astype(bf16)
        .reshape(pair_count, pair_rows, local_heads, head_size)
    )
    d_prob = jnp.einsum("gihd,gjd->ghij", d_out, value_groups, preferred_element_type=f32)
    delta = jnp.sum(probs * d_prob, axis=-1, keepdims=True)
    d_score = (probs * (d_prob - delta) * scale).astype(bf16)
    d_query = (
        jnp.einsum("ghij,gjd->gihd", d_score, key_groups, preferred_element_type=f32)
        .astype(bf16)
        .reshape(row_total, local_heads * head_size)
    )
    d_key = jnp.einsum("ghij,gihd->gjhd", d_score, query_groups, preferred_element_type=f32).astype(
        bf16
    )
    d_value = jnp.einsum("ghij,gihd->gjhd", probs_b, d_out, preferred_element_type=f32).astype(bf16)
    q_grad = contract_first(n_two_b, d_query)
    d_keys = jnp.sum(d_key.astype(f32), axis=2)
    d_values = jnp.sum(d_value.astype(f32), axis=2)
    d_keyval = jnp.concatenate([d_keys, d_values], axis=2).reshape(row_total, 2 * head_size)
    d_keyval_b = d_keyval.astype(bf16)
    kv_own = contract_first(n_two_b, d_keyval_b)
    d_norm_two = contract_last(d_query, q_weight) + contract_last(d_keyval_b, kv_local)
    inner_two_part = jnp.sum(d_query.astype(f32) * query_full, axis=1) + jnp.sum(
        d_keyval * keyval_full, axis=1
    )
    grad_shape = (seq_size, width // seq_size)
    attn_got, norm_two_got, inner_two_got, q_got, kv_got, out_got = exchange(
        5,
        (to_chunks(attn_part, mp_size), "mp", False),
        (to_chunks(d_norm_two.astype(bf16), mp_size), "mp", False),
        (inner_two_part.reshape(slot_count, BLOCK), "mp", True),
        (q_grad.astype(bf16).reshape(grad_shape + q_grad.shape[1:]), "seq", False),
        (kv_own.astype(bf16).reshape(grad_shape + kv_own.shape[1:]), "seq", False),
        (out_grad.astype(bf16).reshape(grad_shape + out_grad.shape[1:]), "seq", False),
    )
    first_in = (moved[0].astype(f32) - live.astype(f32) * total(attn_got)).astype(bf16)
    inner_two = (total(inner_two_got) / width).reshape(row_total, 1)
    n_two_share = second_share.astype(f32) * r_two
    second_cot = (
        moved[3].astype(f32) + (total(norm_two_got) - n_two_share * inner_two) * r_two
    ).astype(bf16)
    (kv_all,) = exchange(6, (total(kv_got), "mp", True))
    kv_share = jnp.stack(
        [
            sum(kv_all[p] for p in range(mp_size) if group_of[p] == g)
            for g in range(kv_count)
        ]
    )
    return (
        first_in,
        second_share,
        first_share,
        second_cot,
        total(q_got),
        kv_share,
        total(out_got).T,
    )


def solution(mesh):
    return jax.shard_map(
        shards,
        mesh=mesh,
        in_specs=(
            P("seq", "mp"),
            P("seq", "mp"),
            P("seq", "mp"),
            P("seq", "mp"),
            P(),
            P(),
            P(),
            P(None, "mp"),
            P(None, "mp", None),
            P("mp", None),
            P(None, None, "mp"),
            P("mp", None),
        ),
        out_specs=(
            P("seq", "mp"),
            P("seq", "mp"),
            P("seq", "mp"),
            P("seq", "mp"),
            P("seq", "mp"),
            P(None, "seq", None),
            P("mp", "seq"),
        ),
        check_vma=False,
    )
```

time: 469 us -> 167 us (0.36)
  waiting for transfers between devices: 312 us -> 0 us
  Pallas kernels: 0 us -> 101 us
  blocking collectives: 41 us -> 0 us
  starting transfers between devices: 40.8 us -> 0 us
  between operations: 14.8 us -> 1.33 us
  other arithmetic: 13 us -> 21.6 us
    reduce_scatter x4 -> x0, waiting for transfers between devices: 212 us -> none  [the longest x1 65.5 us: shards(): lax.psum_scatter(kv_grad, 'seq', scatter_dimension=1, tiled=True)]
    pallas_call x0 -> x7, Pallas kernels: none -> 101 us  [exchange(): pl.pallas_call(functools.partial(exchange_kernel, plans), out_shape=shape...]
    psum x3 -> x0, waiting for transfers between devices: 79 us -> none  [the longest x1 31.8 us: shards(): kv_share = lax.psum(kv_part, 'mp')]
    all_to_all x8 -> x0, starting transfers between devices: 40.5 us -> none  [the longest x4 22.1 us: to_owners(): lax.all_to_all(for_sending(split), 'seq', split_axis=1, concat_axis=0, ti...]
    all_gather x5 -> x0, blocking collectives: 35.2 us -> none  [the longest x1 8.85 us: shards(): lax.all_gather(moved[1], 'mp', axis=1, tiled=True)]
    all_to_all x8 -> x0, waiting for transfers between devices: 20.9 us -> none  [the longest x4 12.2 us: to_owners(): lax.all_to_all(for_sending(split), 'seq', split_axis=1, concat_axis=0, ti...]
    psum x1 -> x0, blocking collectives: 5.75 us -> none  [shards(): lax.psum(jnp.sum(norm_share * n_one_share, axis=1, keepdims=True), 'mp')]
    unnamed x68 -> x78, local copies, waits for them, and re-layouts: 9.81 us -> 9.15 us
  transfers between devices with their start and end apart: 15 -> 0, of which waited for: 12 -> 0; matrix products, arithmetic and copies ran while one was open for 10% -> 0% of each run, Pallas kernels for 0% -> 0%
where the time goes in v1:
time: 167 us; the launch traced here: 166 us
  Pallas kernels  101 us (60%)
  local copies, waits for them, and re-layouts  24 us (14%)
  other arithmetic  21.6 us (13%)
  matrix products  18.5 us (11%)
    pallas_call x7, Pallas kernels, exchange(): pl.pallas_call(functools.partial(exchange_kernel, plans), out_shape=shape...  101 us
    unnamed x78, local copies, waits for them, and re-layouts  9.15 us
    reduce_sum x9, other arithmetic, total(): return jnp.sum(values.astype(jnp.float32), axis=0)  5.14 us
    reshape x4, local copies, waits for them, and re-layouts, to_chunks(): return values.reshape(rows, pieces, width // pieces).transpose(1, 0, 2)  4.04 us
    dot_general x3, matrix products, contract_first(): lax.dot_general(left, right, (((0,), (0,)), ((), ())), preferred_element_...  3.91 us
    dot_general x6, matrix products, contract_last(): lax.dot_general(left, right, (((1,), (1,)), ((), ())), preferred_element_...  3.72 us

profile of v1, /device:TPU:0, one launch (start us, length us, event | category | flops | bytes accessed | tf_op | source)
XLA Modules:
  0.0 166.3 jit_solution(4832246887715123803)
XLA Ops:
  0.7 1.1 copy.106
  1.8 1.0 copy.108
  2.8 1.0 copy.102
  4.0 0.9 pad_maximum_fusion.refs_0_
  5.0 0.7 pad_maximum_fusion.1.refs_1_
  5.7 15.8 %shard_map.171 = (bf16[8,4,2,16,224]{4,3,2,1,0:T(8,128)(2,1)}, bf16[4,224,128]{2,1,0:T(8,128)(2,1)}) custom-call(bf16[8,4,2,16,224]{4,3,2,1,0:T(8,128)(2,1)} %pad_maximum_fusion.refs_0_, bf16[4,224,128]{2,1,0:T(8,128)(2,1)} %pad_maximum_fusion.1.refs_1_), custom_call_target="tpu_custom_call" | custom-call | tf_op jit(solution)/shard_map/pallas_call | solution.py:82
  21.6 2.4 %gather_fusion = bf16[16,4,16,224]{3,2,1,0:T(8,128)(2,1)} fusion(bf16[8,4,2,16,224]{4,3,2,1,0:T(8,128)(2,1)} %get-tuple-element.43, s32[16]{0:T(128)S(1)} %fusion.55), kind=kCustom, calls=%fused_computation | custom fusion | bytes 917632 | tf_op jit(solution)/shard_map/gather | solution.py:190
  24.0 14.6 %shard_map.172 = bf16[8,2,4,16,224]{4,3,2,1,0:T(8,128)(2,1)} custom-call(bf16[8,2,4,16,224]{4,3,2,1,0:T(8,128)(2,1)} %bitcast.221), custom_call_target="tpu_custom_call" | custom-call | tf_op jit(solution)/shard_map/pallas_call | solution.py:82
  38.6 1.2 slice_convert_fusion
  41.1 14.2 %shard_map.173 = (bf16[4,256,224]{2,1,0:T(8,128)(2,1)}, bf16[4,256,224]{2,1,0:T(8,128)(2,1)}) custom-call(bf16[256,224]{1,0:T(8,128)(2,1)} %bitcast.223, bf16[256,224]{1,0:T(8,128)(2,1)} %bitcast.230), custom_call_target="tpu_custom_call" | custom-call | tf_op jit(solution)/shard_map/pallas_call | solution.py:82
  55.4 1.2 fusion.15
  56.6 1.2 fusion.26
  58.0 2.8 %fusion.9 = f32[256,640]{1,0:T(8,128)} fusion(bf16[256,896]{0,1:T(8,128)(2,1)S(1)} %bitcast.243, bf16[2,896,640]{2,1,0:T(8,128)(2,1)} %param.28), kind=kOutput, calls=%fused_computation.27 | convolution fusion | flops 293601280 | bytes 2260992 | tf_op jit(solution)/shard_map/dot_general | solution.py:205
  62.1 2.9 %add_reduce_fusion = (f32[256]{0:T(256)}, f32[256,640]{1,0:T(8,128)S(1)}) fusion(f32[256,640]{1,0:T(8,128)S(1)} %copy-done.32, f32[256,640]{1,0:T(8,128)S(1)} %fusion.69, bf16[256,896]{0,1:T(8,128)(2,1)S(1)} %bitcast.244, bf16[2,896,640]{2,1,0:T(8,128)(2,1)} %param.28), kind=kOutput, calls=%fused_computation.53 | convolution fusion | flops 296713984 | bytes 3572736 | tf_op jit(solution)/shard_map/dot_general | solution.py:206
  65.0 0.8 copy-done.34
  65.8 0.7 fusion.7
  67.4 1.0 copy.118
  68.4 1.7 convolution_convert_fusion
  70.3 1.0 copy.115
  71.3 15.1 %shard_map.174 = (bf16[4,256,224]{2,1,0:T(8,128)(2,1)}, bf16[4,256,224]{2,1,0:T(8,128)(2,1)}, f32[4,2,128]{2,1,0:T(2,128)}) custom-call(bf16[4,256,224]{2,1,0:T(8,128)(2,1)} %bitcast.219, bf16[4,256,224]{2,1,0:T(8,128)(2,1)} %bitcast.218, f32[2,128]{1,0:T(2,128)} %bitcast.253), custom_call_target="tpu_custom_call" | custom-call | tf_op jit(solution)/shard_map/pallas_call | solution.py:82
  86.4 1.2 convert_reduce_fusion.2
  88.3 0.8 fusion.33.refs_1_
  89.2 0.7 fusion.38.refs_0_
  89.9 13.9 %shard_map.175 = (bf16[4,256,224]{2,1,0:T(8,128)(2,1)}, bf16[4,256,224]{2,1,0:T(8,128)(2,1)}) custom-call(bf16[256,224]{1,0:T(8,128)(2,1)} %fusion.38.refs_0_, bf16[256,224]{1,0:T(8,128)(2,1)} %fusion.33.refs_1_), custom_call_target="tpu_custom_call" | custom-call | tf_op jit(solution)/shard_map/pallas_call | solution.py:82
  103.8 1.1 convert_bitcast_fusion
  104.9 1.3 copy.121
  106.4 1.3 fusion.23
  107.7 0.9 fusion.67
  108.8 1.0 fusion.66
  112.2 1.3 fusion.61
  114.8 1.3 select_select_fusion
  117.8 1.0 copy.133
  118.7 2.0 %convolution_convert_fusion.2 = bf16[896,128]{1,0:T(8,128)(2,1)} fusion(bf16[256,896]{0,1:T(8,128)(2,1)} %bitcast.228, bf16[256,128]{0,1:T(8,128)(2,1)S(1)} %bitcast.245), kind=kOutput, calls=%fused_computation.18 | convolution fusion | flops 58834944 | bytes 753664 | tf_op jit(solution)/shard_map/dot_general | solution.py:128
  120.9 0.7 bitcast_multiply_fusion.1
  121.6 1.2 convolution_convert_fusion.5
  123.2 0.7 copy-done.20
  124.6 1.0 convolution_convert_fusion.3
  125.8 1.0 convolution_convert_fusion.4
  128.2 1.0 copy.130
  129.8 1.0 copy.124
  130.8 22.0 %shard_map.176 = (bf16[4,256,224]{2,1,0:T(8,128)(2,1)}, bf16[4,256,224]{2,1,0:T(8,128)(2,1)}, f32[4,2,128]{2,1,0:T(2,128)}, bf16[8,112,128]{2,1,0:T(8,128)(2,1)}...) custom-call(bf16[4,256,224]{2,1,0:T(8,128)(2,1)} %bitcast.217, bf16[4,256,224]{2,1,0:T(8,128)(2,1)} %bitcast.216, ...), custom_call_target="tpu_custom_call" | custom-call | tf_op jit(solution)/shard_map/pallas_call | solution.py:82
  152.9 1.7 %convert_reduce_fusion.5.refs_0_ = f32[112,128]{1,0:T(8,128)} fusion(bf16[8,112,128]{2,1,0:T(8,128)(2,1)} %get-tuple-element.56), kind=kLoop, calls=%fused_computation.69 | loop fusion | flops 215040 | bytes 286720 | tf_op jit(solution)/shard_map/reduce_sum | solution.py:144
  154.5 5.2 %shard_map.177 = f32[4,112,128]{2,1,0:T(8,128)} custom-call(f32[112,128]{1,0:T(8,128)} %convert_reduce_fusion.5.refs_0_), custom_call_target="tpu_custom_call" | custom-call | tf_op jit(solution)/shard_map/pallas_call | solution.py:82
  159.7 1.0 slice_add_fusion.1
  161.7 0.8 copy.137
  162.7 0.8 copy.134
  164.8 0.8 copy.136
  165.5 0.7 copy.135
  (138 shorter events, 16.5 us)
Async XLA Ops:
  0.6 60.4 %copy-start = (bf16[640,896]{1,0:T(8,128)(2,1)S(1)}, bf16[640,896]{1,0:T(8,128)(2,1)}, u32[]{:S(2)}) copy-start(bf16[640,896]{1,0:T(8,128)(2,1)} %param.29) | copy-start | bytes 3440644
  0.6 3.2 %copy-start.25 = (bf16[256,224]{0,1:T(8,128)(2,1)S(1)}, bf16[256,224]{0,1:T(8,128)(2,1)}, u32[]{:S(2)}) copy-start(bf16[256,224]{0,1:T(8,128)(2,1)} %param.19) | copy-start | bytes 344068
  2.8 2.1 %copy-start.18 = (bf16[2,224,128]{2,1,0:T(8,128)(2,1)S(1)}, bf16[2,224,128]{2,1,0:T(8,128)(2,1)}, u32[]{:S(2)}) copy-start(bf16[2,224,128]{2,1,0:T(8,128)(2,1)} %param.26) | copy-start | bytes 344068
  4.0 17.4 %copy-start.31 = (s32[16]{0:T(128)S(1)}, s32[16]{0:T(128)}, u32[]{:S(2)}) copy-start(s32[16]{0:T(128)} %param.24) | copy-start | bytes 196
  58.0 2.8 %copy-start.16 = (bf16[4,256,224]{2,1,0:T(8,128)(2,1)S(1)}, bf16[4,256,224]{2,1,0:T(8,128)(2,1)}, u32[]{:S(2)}) copy-start(bf16[4,256,224]{2,1,0:T(8,128)(2,1)} %get-tuple-element.45) | copy-start | bytes 1376260
  61.0 1.1 copy-start.32
  62.1 3.7 %copy-start.30 = (bf16[2,896,640]{2,1,0:T(8,128)(2,1)S(1)}, bf16[2,896,640]{2,1,0:T(8,128)(2,1)}, u32[]{:S(2)}) copy-start(bf16[2,896,640]{2,1,0:T(8,128)(2,1)} %param.28) | copy-start | bytes 6881284
  65.0 0.8 copy-start.34
  67.1 1.3 copy-start.33
  71.3 17.0 %copy-start.4 = (bf16[1,2,8,16,224]{4,3,2,1,0:T(8,128)(2,1)S(1)}, bf16[1,2,8,16,224]{4,3,2,1,0:T(8,128)(2,1)}, u32[]{:S(2)}) copy-start(bf16[1,2,8,16,224]{4,3,2,1,0:T(8,128)(2,1)} %copy.110) | copy-start | bytes 344068
  86.4 2.7 %copy-start.15 = (bf16[4,256,224]{2,1,0:T(8,128)(2,1)S(1)}, bf16[4,256,224]{2,1,0:T(8,128)(2,1)}, u32[]{:S(2)}) copy-start(bf16[4,256,224]{2,1,0:T(8,128)(2,1)} %get-tuple-element.46) | copy-start | bytes 1376260
  104.9 1.3 copy-start.1
  106.2 1.5 copy-start.8
  107.7 1.1 copy-start.10
  108.6 7.6 %copy-start.19 = (bf16[256,128]{0,1:T(8,128)(2,1)}, bf16[256,128]{0,1:T(8,128)(2,1)S(1)}, u32[]{:S(2)}) copy-start(bf16[256,128]{0,1:T(8,128)(2,1)S(1)} %get-tuple-element.107) | copy-start | bytes 196612
  108.6 1.1 copy-start.28
  108.6 1.5 copy-start.29
  109.8 6.8 %copy-start.23 = (bf16[256,128]{0,1:T(8,128)(2,1)}, bf16[256,128]{0,1:T(8,128)(2,1)S(1)}, u32[]{:S(2)}) copy-start(bf16[256,128]{0,1:T(8,128)(2,1)S(1)} %get-tuple-element.105) | copy-start | bytes 196612
  116.6 1.0 copy-start.3
  116.8 0.5 copy-start.27
  120.7 2.1 %copy-start.24 = (bf16[256,128]{0,1:T(8,128)(2,1)S(1)}, bf16[256,128]{0,1:T(8,128)(2,1)}, u32[]{:S(2)}) copy-start(bf16[256,128]{0,1:T(8,128)(2,1)} %copy-done.23) | copy-start | bytes 196612
  123.1 0.8 copy-start.20
  124.6 2.1 %copy-start.17 = (f32[256,128]{0,1:T(8,128)S(1)}, f32[256,128]{0,1:T(8,128)}, u32[]{:S(2)}) copy-start(f32[256,128]{0,1:T(8,128)} %get-tuple-element.106) | copy-start | bytes 393220
  124.6 2.2 %copy-start.12 = (f32[256,128]{0,1:T(8,128)S(1)}, f32[256,128]{0,1:T(8,128)}, u32[]{:S(2)}) copy-start(f32[256,128]{0,1:T(8,128)} %get-tuple-element.108) | copy-start | bytes 393220
  125.7 1.9 %copy-start.11 = (bf16[4,224,128]{2,1,0:T(8,128)(2,1)S(1)}, bf16[4,224,128]{2,1,0:T(8,128)(2,1)}, u32[]{:S(2)}) copy-start(bf16[4,224,128]{2,1,0:T(8,128)(2,1)} %get-tuple-element.50) | copy-start | bytes 688132
  128.0 1.2 copy-start.9
  152.8 8.5 %copy-start.14 = (bf16[4,256,224]{2,1,0:T(8,128)(2,1)S(1)}, bf16[4,256,224]{2,1,0:T(8,128)(2,1)}, u32[]{:S(2)}) copy-start(bf16[4,256,224]{2,1,0:T(8,128)(2,1)} %get-tuple-element.53) | copy-start | bytes 1376260
  152.8 8.6 %copy-start.26 = (f32[4,2,128]{2,1,0:T(2,128)S(1)}, f32[4,2,128]{2,1,0:T(2,128)}, u32[]{:S(2)}) copy-start(f32[4,2,128]{2,1,0:T(2,128)} %get-tuple-element.54) | copy-start | bytes 12292
  152.9 8.7 %copy-start.2 = (bf16[256,224]{1,0:T(8,128)(2,1)S(1)}, bf16[256,224]{1,0:T(8,128)(2,1)}, u32[]{:S(2)}) copy-start(bf16[256,224]{1,0:T(8,128)(2,1)} %fusion.38.refs_0_) | copy-start | bytes 344068
  152.9 8.7 %copy-start.6 = (bf16[1,2,8,16,224]{4,3,2,1,0:T(8,128)(2,1)S(1)}, bf16[1,2,8,16,224]{4,3,2,1,0:T(8,128)(2,1)}, u32[]{:S(2)}) copy-start(bf16[1,2,8,16,224]{4,3,2,1,0:T(8,128)(2,1)} %copy.112) | copy-start | bytes 344068
  159.7 2.7 %copy-start.13 = (bf16[4,256,224]{2,1,0:T(8,128)(2,1)S(1)}, bf16[4,256,224]{2,1,0:T(8,128)(2,1)}, u32[]{:S(2)}) copy-start(bf16[4,256,224]{2,1,0:T(8,128)(2,1)} %get-tuple-element.52) | copy-start | bytes 1376260
  161.4 1.2 copy-start.5
  161.5 1.9 %copy-start.22 = (bf16[8,112,128]{2,1,0:T(8,128)(2,1)S(1)}, bf16[8,112,128]{2,1,0:T(8,128)(2,1)}, u32[]{:S(2)}) copy-start(bf16[8,112,128]{2,1,0:T(8,128)(2,1)} %get-tuple-element.57) | copy-start | bytes 688132
  161.7 2.4 %copy-start.21 = (bf16[8,112,128]{2,1,0:T(8,128)(2,1)S(1)}, bf16[8,112,128]{2,1,0:T(8,128)(2,1)}, u32[]{:S(2)}) copy-start(bf16[8,112,128]{2,1,0:T(8,128)(2,1)} %get-tuple-element.55) | copy-start | bytes 688132
  161.7 3.0 %copy-start.7 = (bf16[256,224]{1,0:T(8,128)(2,1)S(1)}, bf16[256,224]{1,0:T(8,128)(2,1)}, u32[]{:S(2)}) copy-start(bf16[256,224]{1,0:T(8,128)(2,1)} %fusion.33.refs_1_) | copy-start | bytes 344068

commit v2 on v1

--- a/solution.py
+++ b/solution.py
@@ -22,12 +22,39 @@
         lax.fori_loop(start, stop, lambda k, c: (body(k), c)[1], 0)
 
 
+def near_of(me):
+    return me + 1 - 2 * lax.rem(me, 2)
+
+
+def far_of(me):
+    return lax.rem(me + 2, 4)
+
+
+def remote(source, target, send_sem, recv_sem, axis, peer):
+    return pltpu.make_async_remote_copy(
+        src_ref=source,
+        dst_ref=target,
+        send_sem=send_sem,
+        recv_sem=recv_sem,
+        device_id={axis: peer},
+        device_id_type=pl.DeviceIdType.MESH,
+    )
+
+
 def exchange_kernel(plans, *refs):
     count = len(plans)
     sources, targets = refs[:count], refs[count : 2 * count]
     send_sems = refs[2 * count : 3 * count]
     recv_sems = refs[3 * count : 4 * count]
     own_sem = refs[4 * count]
+    slots = {}
+    rest = list(refs[4 * count + 1 :])
+    for i, (_, _, kind) in enumerate(plans):
+        if kind == "reduce":
+            slots[i] = (rest.pop(0), rest.pop(0))
+    direct = [i for i in range(count) if plans[i][2] in ("send", "gather")]
+    relays = [i for i in range(count) if plans[i][2] == "relay"]
+    reduces = [i for i in range(count) if plans[i][2] == "reduce"]
     barrier = pltpu.get_barrier_semaphore()
     sizes = dict((axis, size) for axis, size, _ in plans)
     for axis, size in sizes.items():
@@ -45,48 +72,111 @@
     pl.semaphore_wait(barrier, sum(size - 1 for size in sizes.values()))
 
     def copy_of(i, k):
-        axis, size, gather = plans[i]
+        axis, size, kind = plans[i]
         me = lax.axis_index(axis)
         peer = lax.rem(me + k, size)
-        return pltpu.make_async_remote_copy(
-            src_ref=sources[i] if gather else sources[i].at[peer],
-            dst_ref=targets[i].at[me],
-            send_sem=send_sems[i].at[k],
-            recv_sem=recv_sems[i].at[k],
-            device_id={axis: peer},
-            device_id_type=pl.DeviceIdType.MESH,
+        source = sources[i] if kind == "gather" else sources[i].at[peer]
+        return remote(
+            source, targets[i].at[me], send_sems[i].at[k], recv_sems[i].at[k], axis, peer
         )
 
     def own_copy(i):
-        axis, _, gather = plans[i]
+        axis, _, kind = plans[i]
         me = lax.axis_index(axis)
-        source = sources[i] if gather else sources[i].at[me]
+        source = sources[i].at[me] if kind == "send" else sources[i]
         return pltpu.make_async_copy(source, targets[i].at[me], own_sem.at[i])
 
-    for i in range(count):
+    def relay_copy(i, k):
+        axis = plans[i][0]
+        me = lax.axis_index(axis)
+        peer = far_of(me) if k == 0 else near_of(me)
+        source = targets[i].at[far_of(me)] if k == 2 else sources[i]
+        target = targets[i].at[far_of(me) if k == 2 else me]
+        return remote(source, target, send_sems[i].at[k], recv_sems[i].at[k], axis, peer)
+
+    def reduce_copy(i, k):
+        axis = plans[i][0]
+        me = lax.axis_index(axis)
+        arrived, staged = slots[i]
+        if k == 2:
+            source, peer = staged, far_of(me)
+        else:
+            peer = near_of(me)
+            source = sources[i].at[far_of(peer) if k == 0 else peer]
+        return remote(source, arrived.at[k], send_sems[i].at[k], recv_sems[i].at[k], axis, peer)
+
+    f32 = jnp.float32
+    for i in relays:
+        relay_copy(i, 0).start()
+    for i in reduces:
+        reduce_copy(i, 0).start()
+    for i in reduces:
+        reduce_copy(i, 1).start()
+    for i in relays:
+        relay_copy(i, 1).start()
+        own_copy(i).start()
+    for i in direct:
         each(1, plans[i][1], lambda k: copy_of(i, k).start())
         own_copy(i).start()
-    for i in range(count):
+    for i in reduces:
+        arrived, staged = slots[i]
+        far = far_of(lax.axis_index(plans[i][0]))
+        reduce_copy(i, 0).wait_recv()
+        staged[...] = (sources[i][far].astype(f32) + arrived[0].astype(f32)).astype(staged.dtype)
+    for i in reduces:
+        reduce_copy(i, 2).start()
+    for i in relays:
+        relay_copy(i, 0).wait_recv()
+        relay_copy(i, 2).start()
+    for i in reduces:
+        arrived, _ = slots[i]
+        me = lax.axis_index(plans[i][0])
+        reduce_copy(i, 1).wait_recv()
+        reduce_copy(i, 2).wait_recv()
+        targets[i][...] = (
+            sources[i][me].astype(f32) + arrived[1].astype(f32) + arrived[2].astype(f32)
+        )
+        for k in range(3):
+            reduce_copy(i, k).wait_send()
+    for i in relays:
+        relay_copy(i, 0).wait_send()
+        relay_copy(i, 1).wait()
+        relay_copy(i, 2).wait()
+        own_copy(i).wait()
+    for i in direct:
         each(1, plans[i][1], lambda k: copy_of(i, k).wait())
         own_copy(i).wait()
 
 
 def exchange(number, *items):
-    plans = tuple((axis, lax.axis_size(axis), gather) for _, axis, gather in items)
-    arrays = [array for array, _, _ in items]
-    shapes = [
-        jax.ShapeDtypeStruct((size,) + (a.shape if gather else a.shape[1:]), a.dtype)
-        for a, (_, size, gather) in zip(arrays, plans)
-    ]
+    plans, shapes, specs, results, buffers = [], [], [], [], []
+    anywhere = pl.BlockSpec(memory_space=pl.ANY)
+    inside = pl.BlockSpec(memory_space=pltpu.VMEM)
+    summed = []
+    for array, axis, kind in items:
+        size = lax.axis_size(axis)
+        summed.append(kind == "reduce" and size != 4)
+        if size != 4:
+            kind = {"relay": "gather", "reduce": "send"}.get(kind, kind)
+        shape, dtype = array.shape, array.dtype
+        if kind in ("relay", "gather"):
+            shape = (size,) + shape
+        if kind == "reduce":
+            shape, dtype = shape[1:], jnp.float32
+            buffers += [pltpu.VMEM((3,) + shape, array.dtype), pltpu.VMEM(shape, array.dtype)]
+        plans.append((axis, size, kind))
+        shapes.append(jax.ShapeDtypeStruct(shape, dtype))
+        specs.append(inside if kind == "reduce" else anywhere)
     sems = [pltpu.SemaphoreType.DMA((size,)) for _, size, _ in plans]
-    return pl.pallas_call(
-        functools.partial(exchange_kernel, plans),
+    results = pl.pallas_call(
+        functools.partial(exchange_kernel, tuple(plans)),
         out_shape=shapes,
-        in_specs=[pl.BlockSpec(memory_space=pl.ANY)] * len(arrays),
-        out_specs=[pl.BlockSpec(memory_space=pl.ANY)] * len(arrays),
-        scratch_shapes=sems + sems + [pltpu.SemaphoreType.DMA((len(arrays),))],
+        in_specs=specs,
+        out_specs=specs,
+        scratch_shapes=sems + sems + [pltpu.SemaphoreType.DMA((len(plans),))] + buffers,
         compiler_params=pltpu.CompilerParams(collective_id=number, has_side_effects=True),
-    )(*arrays)
+    )(*[array for array, _, _ in items])
+    return [total(r) if add else r for r, add in zip(results, summed)]
 
 
 def normalize(values):
@@ -177,22 +267,34 @@
     per_group = local_heads * mp_size // kv_count
     group_of = [p * local_heads // per_group for p in range(mp_size)]
 
-    streams = jnp.stack(
-        [
-            item.reshape(slot_count, seq_size, share_rows, share_width).transpose(1, 0, 2, 3)
-            for item in (y_first, y_second, grad_first, grad_second)
-        ],
-        axis=1,
-    )
+    def to_shares(*values):
+        return jnp.stack(
+            [
+                item.reshape(slot_count, seq_size, share_rows, share_width).transpose(1, 0, 2, 3)
+                for item in values
+            ],
+            axis=1,
+        )
+
+    def to_slots(held):
+        placed = held[source // slot_count, :, source % slot_count]
+        return placed.reshape(seq_size, slot_count, held.shape[1], share_rows, share_width)
+
+    def from_shares(owned):
+        moved = owned.transpose(2, 1, 0, 3, 4)
+        return moved.reshape(owned.shape[2], row_total, share_width)
+
     kv_sent = jnp.stack([kv_weight[g] for g in group_of])
-    held, kv_parts = exchange(0, (streams, "seq", False), (kv_sent, "mp", False))
+    first_all, cot_second_all, held, kv_parts = exchange(
+        0,
+        (y_first, "mp", "relay"),
+        (grad_second, "mp", "relay"),
+        (to_shares(y_first, grad_second), "seq", "send"),
+        (kv_sent, "mp", "send"),
+    )
     kv_local = kv_parts.reshape(width, 2 * head_size)
-    placed = held[source // slot_count, :, source % slot_count]
-    placed = placed.reshape(seq_size, slot_count, 4, share_rows, share_width)
-    (owned,) = exchange(1, (placed, "seq", False))
-    moved = owned.transpose(2, 1, 0, 3, 4).reshape(4, row_total, share_width)
-    gathered = exchange(2, (moved[0], "mp", True), (moved[3], "mp", True))
-    first, cot_second = (from_chunks(item) for item in gathered)
+    first = from_chunks(first_all)
+    cot_second = from_chunks(cot_second_all)
 
     owned_slots = lax.axis_index("seq") * slot_count + jnp.arange(slot_count, dtype=jnp.int32)
     mine = source[owned_slots]
@@ -213,19 +315,24 @@
     d_up = (d_hidden * silu_gate).astype(bf16)
     norm_part = contract_last(d_gate, gate_up[0]) + contract_last(d_up, gate_up[1])
     inner_part = jnp.sum(d_gate.astype(f32) * gate_pre + d_up.astype(f32) * up_pre, axis=1)
-    mix_got, norm_got, inner_got = exchange(
-        3,
-        (to_chunks(mix_part, mp_size), "mp", False),
-        (to_chunks(norm_part.astype(bf16), mp_size), "mp", False),
-        (inner_part.reshape(slot_count, BLOCK), "mp", True),
-    )
-    second_share = (moved[1].astype(f32) - total(mix_got)).astype(bf16)
+    mixed, norm_share, inner_got, owned = exchange(
+        1,
+        (to_chunks(mix_part, mp_size), "mp", "reduce"),
+        (to_chunks(norm_part.astype(bf16), mp_size), "mp", "reduce"),
+        (inner_part.reshape(slot_count, BLOCK), "mp", "gather"),
+        (to_slots(held), "seq", "send"),
+    )
+    first_own, cot_second_own = from_shares(owned)
+    second_pack = (y_second.astype(f32) - mixed).astype(bf16)
     inner = (total(inner_got) / width).reshape(row_total, 1)
-    n_one_share = moved[0].astype(f32) * r_one
-    first_share = (
-        moved[2].astype(f32) + (total(norm_got) - n_one_share * inner) * r_one
+    n_one_share = y_first.astype(f32) * r_one
+    first_pack = (
+        grad_first.astype(f32) + (norm_share - n_one_share * inner) * r_one
     ).astype(bf16)
-    second_all, cot_all = exchange(4, (second_share, "mp", True), (first_share, "mp", True))
+    (held,) = exchange(2, (to_shares(second_pack, first_pack), "seq", "send"))
+    (owned,) = exchange(3, (to_slots(held), "seq", "send"))
+    second_share, first_share = from_shares(owned)
+    second_all, cot_all = exchange(4, (second_share, "mp", "relay"), (first_share, "mp", "relay"))
     second_in = from_chunks(second_all)
     first_cot = from_chunks(cot_all)
 
@@ -289,22 +396,23 @@
         d_keyval * keyval_full, axis=1
     )
     grad_shape = (seq_size, width // seq_size)
-    attn_got, norm_two_got, inner_two_got, q_got, kv_got, out_got = exchange(
+    attn, norm_two_share, inner_two_got, q_got, kv_got, out_got = exchange(
         5,
-        (to_chunks(attn_part, mp_size), "mp", False),
-        (to_chunks(d_norm_two.astype(bf16), mp_size), "mp", False),
-        (inner_two_part.reshape(slot_count, BLOCK), "mp", True),
-        (q_grad.astype(bf16).reshape(grad_shape + q_grad.shape[1:]), "seq", False),
-        (kv_own.astype(bf16).reshape(grad_shape + kv_own.shape[1:]), "seq", False),
-        (out_grad.astype(bf16).reshape(grad_shape + out_grad.shape[1:]), "seq", False),
-    )
-    first_in = (moved[0].astype(f32) - live.astype(f32) * total(attn_got)).astype(bf16)
+        (to_chunks(attn_part, mp_size), "mp", "reduce"),
+        (to_chunks(d_norm_two.astype(bf16), mp_size), "mp", "reduce"),
+        (inner_two_part.reshape(slot_count, BLOCK), "mp", "gather"),
+        (q_grad.astype(bf16).reshape(grad_shape + q_grad.shape[1:]), "seq", "send"),
+        (kv_own.astype(bf16).reshape(grad_shape + kv_own.shape[1:]), "seq", "send"),
+        (out_grad.astype(bf16).reshape(grad_shape + out_grad.shape[1:]), "seq", "send"),
+    )
+    first_in = (first_own.astype(f32) - live.astype(f32) * attn).astype(bf16)
     inner_two = (total(inner_two_got) / width).reshape(row_total, 1)
     n_two_share = second_share.astype(f32) * r_two
     second_cot = (
-        moved[3].astype(f32) + (total(norm_two_got) - n_two_share * inner_two) * r_two
+        cot_second_own.astype(f32) + (norm_two_share - n_two_share * inner_two) * r_two
     ).astype(bf16)
-    (kv_all,) = exchange(6, (total(kv_got), "mp", True))
+    (kv_all,) = exchange(6, (total(kv_got).astype(bf16), "mp", "relay"))
+    kv_all = kv_all.astype(f32)
     kv_share = jnp.stack(
         [
             sum(kv_all[p] for p in range(mp_size) if group_of[p] == g)

time: 167 us -> 151 us (0.904)
  Pallas kernels: 101 us -> 87.9 us
  other arithmetic: 21.6 us -> 19.2 us
    pallas_call x7, Pallas kernels: 101 us -> 87.9 us  [exchange(): pl.pallas_call(functools.partial(exchange_kernel, tuple(plans)), out_shap...]
    another operation x2 -> x4, local copies, waits for them, and re-layouts: 0.04 us -> 2.33 us  [the longest x3 2.31 us: shards(): second_share, first_share = from_shares(owned)]
    unnamed x78 -> x80, local copies, waits for them, and re-layouts: 9.15 us -> 7.17 us
    reduce_sum x9 -> x5, other arithmetic: 5.14 us -> 3.65 us  [total(): return jnp.sum(values.astype(jnp.float32), axis=0)]
    gather x1 -> x2, local copies, waits for them, and re-layouts: 2.44 us -> 3.52 us  [to_slots(): placed = held[source // slot_count, :, source % slot_count]]
    convert_element_type x6 -> x7, other arithmetic: 4.22 us -> 3.69 us  [the longest x2 1.41 us: shards(): first_in = (first_own.astype(f32) - live.astype(f32) * attn).astype(bf16)]
where the time goes in v2:
time: 151 us; the launch traced here: 150 us
  Pallas kernels  87.9 us (58%)
  local copies, waits for them, and re-layouts  24.2 us (16%)
  other arithmetic  19.2 us (13%)
  matrix products  17.6 us (12%)
    pallas_call x7, Pallas kernels, exchange(): pl.pallas_call(functools.partial(exchange_kernel, tuple(plans)), out_shap...  87.9 us
    unnamed x80, local copies, waits for them, and re-layouts  7.17 us
    reshape x4, local copies, waits for them, and re-layouts, to_chunks(): return values.reshape(rows, pieces, width // pieces).transpose(1, 0, 2)  4.04 us
    dot_general x3, matrix products, contract_first(): lax.dot_general(left, right, (((0,), (0,)), ((), ())), preferred_element_...  3.93 us
    dot_general x6, matrix products, contract_last(): lax.dot_general(left, right, (((1,), (1,)), ((), ())), preferred_element_...  3.7 us
    reduce_sum x5, other arithmetic, total(): return jnp.sum(values.astype(jnp.float32), axis=0)  3.65 us
    gather x2, local copies, waits for them, and re-layouts, to_slots(): placed = held[source // slot_count, :, source % slot_count]  3.52 us

profile of v2, /device:TPU:0, one launch (start us, length us, event | category | flops | bytes accessed | tf_op | source)
XLA Modules:
  0.0 150.3 jit_solution(6702882962308096387)
XLA Ops:
  0.7 1.1 copy.117.refs_0_
  1.8 1.0 copy.118.refs_1_
  2.9 0.7 pad_maximum_fusion.refs_2_
  3.6 0.7 pad_maximum_fusion.2.refs_3_
  4.4 18.2 %shard_map.171 = (bf16[4,256,224]{2,1,0:T(8,128)(2,1)}, bf16[4,256,224]{2,1,0:T(8,128)(2,1)}, bf16[8,2,2,16,224]{4,3,2,1,0:T(8,128)(2,1)}, bf16[4,224,128]{2,1,0:T(8,128)(2,1)}) custom-call(bf16[256,224]{1,0:T(8,128)(2,1)} %copy-done.4, bf16[256,224]{1,0:T(8,128)(2,1)} %copy-done.7, bf16[8,2,2,16,224]{4,3,2,1,0:T(8,128)(2,1)} %pad_maximum_fusion.refs_2_, ...), custom_call_target="tpu_custom_call" | custom-call | tf_op jit(solution)/shard_map/pallas_call | solution.py:171
  22.6 1.2 fusion.15
  23.8 1.2 fusion.26
  25.2 1.9 %fusion.9 = f32[256,640]{1,0:T(8,128)S(1)} fusion(bf16[256,896]{0,1:T(8,128)(2,1)S(1)} %bitcast.252, bf16[2,896,640]{2,1,0:T(8,128)(2,1)} %param.28), kind=kOutput, calls=%fused_computation.28 | convolution fusion | flops 293601280 | bytes 2260992 | tf_op jit(solution)/shard_map/dot_general | solution.py:307
  28.0 2.9 %add_reduce_fusion = (f32[256]{0:T(256)}, f32[256,640]{1,0:T(8,128)S(1)}) fusion(f32[256,640]{1,0:T(8,128)S(1)} %fusion.9, f32[256,640]{1,0:T(8,128)S(1)} %fusion.65, bf16[256,896]{0,1:T(8,128)(2,1)S(1)} %bitcast.253, bf16[2,896,640]{2,1,0:T(8,128)(2,1)} %param.28), kind=kOutput, calls=%fused_computation.50 | convolution fusion | flops 296713984 | bytes 3572736 | tf_op jit(solution)/shard_map/dot_general | solution.py:308
  30.9 0.7 fusion.7
  32.6 1.0 copy.124
  33.6 1.7 %convolution_convert_fusion = bf16[256,896]{1,0:T(8,128)(2,1)S(1)} fusion(bf16[640,896]{1,0:T(8,128)(2,1)S(1)} %copy-done, f32[256,640]{1,0:T(8,128)} %copy-done.35, f32[256,640]{1,0:T(8,128)S(1)} %fusion.9), kind=kOutput, calls=%fused_computation.14 | convolution fusion | flops 294813696 | bytes 2916352 | tf_op jit(solution)/shard_map/dot_general | solution.py:312
  35.5 1.0 copy.121
  36.7 1.3 gather_fusion
  38.0 12.6 %shard_map.172 = (f32[256,224]{1,0:T(8,128)}, f32[256,224]{1,0:T(8,128)}, f32[4,2,128]{2,1,0:T(2,128)}, bf16[8,2,2,16,224]{4,3,2,1,0:T(8,128)(2,1)}) custom-call(bf16[4,256,224]{2,1,0:T(8,128)(2,1)} %bitcast.223, bf16[4,256,224]{2,1,0:T(8,128)(2,1)} %bitcast.222, f32[2,128]{1,0:T(2,128)} %bitcast.263, bf16[8,2,2,16,224]{4,3,2,1,0:T(8,128)(2,1)} %bitcast.241), custom_call_target="tpu_custom_call" | custom-call | tf_op jit(solution)/shard_map/pallas_call | solution.py:171
  50.6 0.7 reduce_sum.192
  51.5 1.1 add_convert_fusion
  52.8 0.7 pad_maximum_fusion.1.refs_0_
  53.5 9.3 %shard_map.173 = bf16[8,2,2,16,224]{4,3,2,1,0:T(8,128)(2,1)} custom-call(bf16[8,2,2,16,224]{4,3,2,1,0:T(8,128)(2,1)} %pad_maximum_fusion.1.refs_0_), custom_call_target="tpu_custom_call" | custom-call | tf_op jit(solution)/shard_map/pallas_call | solution.py:171
  62.8 2.2 %gather_fusion.3 = bf16[16,2,16,224]{3,2,1,0:T(8,128)(2,1)} fusion(bf16[8,2,2,16,224]{4,3,2,1,0:T(8,128)(2,1)} %shard_map.173, s32[16]{0:T(128)S(1)} %fusion.50), kind=kCustom, calls=%fused_computation.3 | custom fusion | bytes 458880 | tf_op jit(solution)/shard_map/gather | solution.py:280
  65.0 9.8 %shard_map.174 = bf16[8,2,2,16,224]{4,3,2,1,0:T(8,128)(2,1)} custom-call(bf16[8,2,2,16,224]{4,3,2,1,0:T(8,128)(2,1)} %bitcast.240), custom_call_target="tpu_custom_call" | custom-call | tf_op jit(solution)/shard_map/pallas_call | solution.py:171
  74.9 1.0 fusion.58
  76.5 0.7 copy.132
  77.2 10.4 %shard_map.175 = (bf16[4,256,224]{2,1,0:T(8,128)(2,1)}, bf16[4,256,224]{2,1,0:T(8,128)(2,1)}) custom-call(bf16[256,224]{1,0:T(8,128)(2,1)} %bitcast.225, bf16[256,224]{1,0:T(8,128)(2,1)} %bitcast.234), custom_call_target="tpu_custom_call" | custom-call | tf_op jit(solution)/shard_map/pallas_call | solution.py:171
  87.6 1.1 convert_bitcast_fusion
  88.8 1.3 copy.134
  90.2 1.3 fusion.23
  91.5 0.9 fusion.63
  92.6 1.0 fusion.62
  96.1 1.3 fusion.56
  98.6 1.3 select_select_fusion
  101.6 1.0 copy.146
  102.6 2.0 %convolution_convert_fusion.2 = bf16[896,128]{1,0:T(8,128)(2,1)} fusion(bf16[256,896]{0,1:T(8,128)(2,1)} %bitcast.232, bf16[256,128]{0,1:T(8,128)(2,1)S(1)} %bitcast.255), kind=kOutput, calls=%fused_computation.19 | convolution fusion | flops 58834944 | bytes 753664 | tf_op jit(solution)/shard_map/dot_general | solution.py:218
  104.8 0.7 bitcast_multiply_fusion.1
  105.5 1.2 convolution_convert_fusion.5
  107.1 0.7 copy-done.22
  108.4 1.0 convolution_convert_fusion.3
  109.6 1.0 convolution_convert_fusion.4
  112.1 1.0 copy.143
  113.6 1.0 copy.137
  114.7 22.1 %shard_map.176 = (f32[256,224]{1,0:T(8,128)}, f32[256,224]{1,0:T(8,128)}, f32[4,2,128]{2,1,0:T(2,128)}, bf16[8,112,128]{2,1,0:T(8,128)(2,1)}, bf16[8,112,128]{2,...) custom-call(bf16[4,256,224]{2,1,0:T(8,128)(2,1)} %bitcast.221, bf16[4,256,224]{2,1,0:T(8,128)(2,1)} %bitcast.220, ...), custom_call_target="tpu_custom_call" | custom-call | tf_op jit(solution)/shard_map/pallas_call | solution.py:171
  136.8 1.6 %reduce_sum.206.refs_0_ = bf16[112,128]{1,0:T(8,128)(2,1)} reduce(bf16[8,112,128]{2,1,0:T(8,128)(2,1)} %get-tuple-element.58, bf16[]{:T(256)} %constant.170.clone.1), dimensions={0}, to_apply=%region_19.21 | reduce | flops 100352 | bytes 258050 | tf_op jit(solution)/shard_map/reduce_sum | solution.py:234
  138.4 5.5 %shard_map.177 = bf16[4,112,128]{2,1,0:T(8,128)(2,1)} custom-call(bf16[112,128]{1,0:T(8,128)(2,1)} %reduce_sum.206.refs_0_), custom_call_target="tpu_custom_call" | custom-call | tf_op jit(solution)/shard_map/pallas_call | solution.py:171
  143.9 1.0 convert_element_type.259
  145.8 0.8 copy.151
  146.7 0.8 copy.148
  148.8 0.7 copy.149
  149.6 0.8 copy.150
  (141 shorter events, 14.9 us)
Async XLA Ops:
  0.6 26.7 %copy-start = (bf16[640,896]{1,0:T(8,128)(2,1)S(1)}, bf16[640,896]{1,0:T(8,128)(2,1)}, u32[]{:S(2)}) copy-start(bf16[640,896]{1,0:T(8,128)(2,1)} %param.29) | copy-start | bytes 3440644
  0.6 3.0 %copy-start.15 = (bf16[2,224,128]{2,1,0:T(8,128)(2,1)S(1)}, bf16[2,224,128]{2,1,0:T(8,128)(2,1)}, u32[]{:S(2)}) copy-start(bf16[2,224,128]{2,1,0:T(8,128)(2,1)} %param.26) | copy-start | bytes 344068
  1.8 2.6 %copy-start.4 = (bf16[256,224]{1,0:T(8,128)(2,1)}, bf16[256,224]{1,0:T(8,128)(2,1)S(1)}, u32[]{:S(2)}) copy-start(bf16[256,224]{1,0:T(8,128)(2,1)S(1)} %copy.117.refs_0_) | copy-start | bytes 344068
  2.8 1.5 %copy-start.7 = (bf16[256,224]{1,0:T(8,128)(2,1)}, bf16[256,224]{1,0:T(8,128)(2,1)S(1)}, u32[]{:S(2)}) copy-start(bf16[256,224]{1,0:T(8,128)(2,1)S(1)} %copy.118.refs_1_) | copy-start | bytes 344068
  25.2 1.9 %copy-start.13 = (bf16[4,256,224]{2,1,0:T(8,128)(2,1)S(1)}, bf16[4,256,224]{2,1,0:T(8,128)(2,1)}, u32[]{:S(2)}) copy-start(bf16[4,256,224]{2,1,0:T(8,128)(2,1)} %get-tuple-element.45) | copy-start | bytes 1376260
  28.0 2.9 %copy-start.33 = (bf16[2,896,640]{2,1,0:T(8,128)(2,1)S(1)}, bf16[2,896,640]{2,1,0:T(8,128)(2,1)}, u32[]{:S(2)}) copy-start(bf16[2,896,640]{2,1,0:T(8,128)(2,1)} %param.28) | copy-start | bytes 6881284
  30.9 0.9 copy-start.35
  35.3 1.3 copy-start.34
  35.3 1.4 copy-start.19
  36.5 14.8 %copy-start.27 = (bf16[256,224]{0,1:T(8,128)(2,1)S(1)}, bf16[256,224]{0,1:T(8,128)(2,1)}, u32[]{:S(2)}) copy-start(bf16[256,224]{0,1:T(8,128)(2,1)} %param.20) | copy-start | bytes 344068
  36.5 14.9 %copy-start.5 = (bf16[256,224]{1,0:T(8,128)(2,1)S(1)}, bf16[256,224]{1,0:T(8,128)(2,1)}, u32[]{:S(2)}) copy-start(bf16[256,224]{1,0:T(8,128)(2,1)} %copy-done.4) | copy-start | bytes 344068
  38.0 14.6 %copy-start.28 = (bf16[256,224]{0,1:T(8,128)(2,1)S(1)}, bf16[256,224]{0,1:T(8,128)(2,1)}, u32[]{:S(2)}) copy-start(bf16[256,224]{0,1:T(8,128)(2,1)} %param.19) | copy-start | bytes 344068
  50.6 2.1 %copy-start.20 = (f32[256,224]{1,0:T(8,128)S(1)}, f32[256,224]{1,0:T(8,128)}, u32[]{:S(2)}) copy-start(f32[256,224]{1,0:T(8,128)} %get-tuple-element.48) | copy-start | bytes 688132
  88.7 1.3 copy-start.1
  90.0 1.5 copy-start.8
  91.5 1.1 copy-start.10
  92.4 7.6 %copy-start.21 = (bf16[256,128]{0,1:T(8,128)(2,1)}, bf16[256,128]{0,1:T(8,128)(2,1)S(1)}, u32[]{:S(2)}) copy-start(bf16[256,128]{0,1:T(8,128)(2,1)S(1)} %get-tuple-element.109) | copy-start | bytes 196612
  92.4 1.1 copy-start.31
  92.5 1.5 copy-start.32
  93.6 6.8 %copy-start.25 = (bf16[256,128]{0,1:T(8,128)(2,1)}, bf16[256,128]{0,1:T(8,128)(2,1)S(1)}, u32[]{:S(2)}) copy-start(bf16[256,128]{0,1:T(8,128)(2,1)S(1)} %get-tuple-element.107) | copy-start | bytes 196612
  100.4 1.0 copy-start.2
  100.7 0.5 copy-start.30
  104.6 2.1 %copy-start.26 = (bf16[256,128]{0,1:T(8,128)(2,1)S(1)}, bf16[256,128]{0,1:T(8,128)(2,1)}, u32[]{:S(2)}) copy-start(bf16[256,128]{0,1:T(8,128)(2,1)} %copy-done.25) | copy-start | bytes 196612
  106.9 0.8 copy-start.22
  108.4 2.1 %copy-start.14 = (f32[256,128]{0,1:T(8,128)S(1)}, f32[256,128]{0,1:T(8,128)}, u32[]{:S(2)}) copy-start(f32[256,128]{0,1:T(8,128)} %get-tuple-element.108) | copy-start | bytes 393220
  108.4 2.2 %copy-start.12 = (f32[256,128]{0,1:T(8,128)S(1)}, f32[256,128]{0,1:T(8,128)}, u32[]{:S(2)}) copy-start(f32[256,128]{0,1:T(8,128)} %get-tuple-element.110) | copy-start | bytes 393220
  109.6 1.9 %copy-start.11 = (bf16[4,224,128]{2,1,0:T(8,128)(2,1)S(1)}, bf16[4,224,128]{2,1,0:T(8,128)(2,1)}, u32[]{:S(2)}) copy-start(bf16[4,224,128]{2,1,0:T(8,128)(2,1)} %get-tuple-element.52) | copy-start | bytes 688132
  111.8 1.3 copy-start.9
  114.7 30.9 %copy-start.16 = (bf16[8,2,2,16,224]{4,3,2,1,0:T(8,128)(2,1)S(1)}, bf16[8,2,2,16,224]{4,3,2,1,0:T(8,128)(2,1)}, u32[]{:S(2)}) copy-start(bf16[8,2,2,16,224]{4,3,2,1,0:T(8,128)(2,1)} %get-tuple-element.47) | copy-start | bytes 688132
  136.8 8.7 %copy-start.29 = (f32[4,2,128]{2,1,0:T(2,128)S(1)}, f32[4,2,128]{2,1,0:T(2,128)}, u32[]{:S(2)}) copy-start(f32[4,2,128]{2,1,0:T(2,128)} %get-tuple-element.56) | copy-start | bytes 12292
  143.9 1.8 %copy-start.3 = (bf16[1,2,8,16,224]{4,3,2,1,0:T(8,128)(2,1)S(1)}, bf16[1,2,8,16,224]{4,3,2,1,0:T(8,128)(2,1)}, u32[]{:S(2)}) copy-start(bf16[1,2,8,16,224]{4,3,2,1,0:T(8,128)(2,1)} %copy.131) | copy-start | bytes 344068
  143.9 1.8 %copy-start.18 = (f32[256,224]{1,0:T(8,128)S(1)}, f32[256,224]{1,0:T(8,128)}, u32[]{:S(2)}) copy-start(f32[256,224]{1,0:T(8,128)} %get-tuple-element.55) | copy-start | bytes 688132
  145.6 1.0 copy-start.17
  145.7 1.8 %copy-start.24 = (bf16[8,112,128]{2,1,0:T(8,128)(2,1)S(1)}, bf16[8,112,128]{2,1,0:T(8,128)(2,1)}, u32[]{:S(2)}) copy-start(bf16[8,112,128]{2,1,0:T(8,128)(2,1)} %get-tuple-element.59) | copy-start | bytes 688132
  145.8 2.3 %copy-start.23 = (bf16[8,112,128]{2,1,0:T(8,128)(2,1)S(1)}, bf16[8,112,128]{2,1,0:T(8,128)(2,1)}, u32[]{:S(2)}) copy-start(bf16[8,112,128]{2,1,0:T(8,128)(2,1)} %get-tuple-element.57) | copy-start | bytes 688132
  146.6 3.0 %copy-start.6 = (bf16[1,2,8,16,224]{4,3,2,1,0:T(8,128)(2,1)S(1)}, bf16[1,2,8,16,224]{4,3,2,1,0:T(8,128)(2,1)}, u32[]{:S(2)}) copy-start(bf16[1,2,8,16,224]{4,3,2,1,0:T(8,128)(2,1)} %copy.132) | copy-start | bytes 344068

commit v3 on v2

--- a/solution.py
+++ b/solution.py
@@ -50,11 +50,12 @@
     slots = {}
     rest = list(refs[4 * count + 1 :])
     for i, (_, _, kind) in enumerate(plans):
-        if kind == "reduce":
+        if kind in ("reduce", "pair"):
             slots[i] = (rest.pop(0), rest.pop(0))
     direct = [i for i in range(count) if plans[i][2] in ("send", "gather")]
     relays = [i for i in range(count) if plans[i][2] == "relay"]
     reduces = [i for i in range(count) if plans[i][2] == "reduce"]
+    pairs = [i for i in range(count) if plans[i][2] == "pair"]
     barrier = pltpu.get_barrier_semaphore()
     sizes = dict((axis, size) for axis, size, _ in plans)
     for axis, size in sizes.items():
@@ -105,7 +106,36 @@
             source = sources[i].at[far_of(peer) if k == 0 else peer]
         return remote(source, arrived.at[k], send_sems[i].at[k], recv_sems[i].at[k], axis, peer)
 
+    def near_copy(i, j):
+        axis = plans[i][0]
+        near = near_of(lax.axis_index(axis))
+        arrived, _ = slots[i]
+        return remote(
+            sources[i].at[2 * j + lax.rem(near, 2)],
+            arrived.at[j],
+            send_sems[i].at[2 * j],
+            recv_sems[i].at[2 * j],
+            axis,
+            near,
+        )
+
+    def pair_copy(i, k):
+        axis, size, _ = plans[i]
+        me = lax.axis_index(axis)
+        peer = lax.rem(me + 2 * k, size)
+        _, staged = slots[i]
+        return remote(
+            staged.at[peer // 2],
+            targets[i].at[me // 2],
+            send_sems[i].at[2 * k + 1],
+            recv_sems[i].at[2 * k + 1],
+            axis,
+            peer,
+        )
+
     f32 = jnp.float32
+    for i in pairs:
+        each(0, plans[i][1] // 2, lambda j: near_copy(i, j).start())
     for i in relays:
         relay_copy(i, 0).start()
     for i in reduces:
@@ -128,6 +158,24 @@
     for i in relays:
         relay_copy(i, 0).wait_recv()
         relay_copy(i, 2).start()
+    for i in pairs:
+        arrived, staged = slots[i]
+        half = plans[i][1] // 2
+        me = lax.axis_index(plans[i][0])
+
+        def add(j):
+            near_copy(i, j).wait_recv()
+            own = sources[i][2 * j + lax.rem(me, 2)].astype(f32)
+            staged[j] = (own + arrived[j].astype(f32)).astype(staged.dtype)
+
+        each(0, half, add)
+        each(1, half, lambda k: pair_copy(i, k).start())
+    for i in pairs:
+        half = plans[i][1] // 2
+        me = lax.axis_index(plans[i][0])
+        targets[i][me // 2] = slots[i][1][me // 2]
+        each(1, half, lambda k: pair_copy(i, k).wait())
+        each(0, half, lambda j: near_copy(i, j).wait_send())
     for i in reduces:
         arrived, _ = slots[i]
         me = lax.axis_index(plans[i][0])
@@ -159,14 +207,19 @@
         if size != 4:
             kind = {"relay": "gather", "reduce": "send"}.get(kind, kind)
         shape, dtype = array.shape, array.dtype
+        if kind == "pair" and size % 2:
+            kind = "send"
         if kind in ("relay", "gather"):
             shape = (size,) + shape
+        if kind == "pair":
+            shape = (size // 2,) + shape[1:]
+            buffers += [pltpu.VMEM(shape, dtype), pltpu.VMEM(shape, dtype)]
         if kind == "reduce":
             shape, dtype = shape[1:], jnp.float32
             buffers += [pltpu.VMEM((3,) + shape, array.dtype), pltpu.VMEM(shape, array.dtype)]
         plans.append((axis, size, kind))
         shapes.append(jax.ShapeDtypeStruct(shape, dtype))
-        specs.append(inside if kind == "reduce" else anywhere)
+        specs.append(inside if kind in ("reduce", "pair") else anywhere)
     sems = [pltpu.SemaphoreType.DMA((size,)) for _, size, _ in plans]
     results = pl.pallas_call(
         functools.partial(exchange_kernel, tuple(plans)),
@@ -285,21 +338,21 @@
         return moved.reshape(owned.shape[2], row_total, share_width)
 
     kv_sent = jnp.stack([kv_weight[g] for g in group_of])
-    first_all, cot_second_all, held, kv_parts = exchange(
+    first_all, cot_second_all, held = exchange(
         0,
         (y_first, "mp", "relay"),
         (grad_second, "mp", "relay"),
         (to_shares(y_first, grad_second), "seq", "send"),
-        (kv_sent, "mp", "send"),
-    )
-    kv_local = kv_parts.reshape(width, 2 * head_size)
+    )
     first = from_chunks(first_all)
     cot_second = from_chunks(cot_second_all)
 
     owned_slots = lax.axis_index("seq") * slot_count + jnp.arange(slot_count, dtype=jnp.int32)
-    mine = source[owned_slots]
-    row_doc = jnp.repeat(owner_doc[mine], BLOCK, total_repeat_length=row_total)
-    row_limit = jnp.repeat(limit[mine], BLOCK, total_repeat_length=row_total)
+    mine = (plan[None, :] == owned_slots[:, None]).astype(jnp.int32)
+    slot_doc = jnp.sum(mine * owner_doc[None, :], axis=1)
+    slot_limit = jnp.sum(mine * limit[None, :], axis=1)
+    row_doc = jnp.broadcast_to(slot_doc[:, None], (slot_count, BLOCK)).reshape(row_total)
+    row_limit = jnp.broadcast_to(slot_limit[:, None], (slot_count, BLOCK)).reshape(row_total)
     valid = jnp.arange(row_total, dtype=jnp.int32) % BLOCK < row_limit
 
     n_one, r_one = normalize(first.astype(f32))
@@ -329,7 +382,10 @@
     first_pack = (
         grad_first.astype(f32) + (norm_share - n_one_share * inner) * r_one
     ).astype(bf16)
-    (held,) = exchange(2, (to_shares(second_pack, first_pack), "seq", "send"))
+    held, kv_parts = exchange(
+        2, (to_shares(second_pack, first_pack), "seq", "send"), (kv_sent, "mp", "send")
+    )
+    kv_local = kv_parts.reshape(width, 2 * head_size)
     (owned,) = exchange(3, (to_slots(held), "seq", "send"))
     second_share, first_share = from_shares(owned)
     second_all, cot_all = exchange(4, (second_share, "mp", "relay"), (first_share, "mp", "relay"))
@@ -401,9 +457,9 @@
         (to_chunks(attn_part, mp_size), "mp", "reduce"),
         (to_chunks(d_norm_two.astype(bf16), mp_size), "mp", "reduce"),
         (inner_two_part.reshape(slot_count, BLOCK), "mp", "gather"),
-        (q_grad.astype(bf16).reshape(grad_shape + q_grad.shape[1:]), "seq", "send"),
-        (kv_own.astype(bf16).reshape(grad_shape + kv_own.shape[1:]), "seq", "send"),
-        (out_grad.astype(bf16).reshape(grad_shape + out_grad.shape[1:]), "seq", "send"),
+        (q_grad.astype(bf16).reshape(grad_shape + q_grad.shape[1:]), "seq", "pair"),
+        (kv_own.astype(bf16).reshape(grad_shape + kv_own.shape[1:]), "seq", "pair"),
+        (out_grad.astype(bf16).reshape(grad_shape + out_grad.shape[1:]), "seq", "pair"),
     )
     first_in = (first_own.astype(f32) - live.astype(f32) * attn).astype(bf16)
     inner_two = (total(inner_two_got) / width).reshape(row_total, 1)

time: 151 us -> 142 us (0.940)
  Pallas kernels: 87.9 us -> 84 us
  other arithmetic: 19.2 us -> 16.8 us
  local copies, waits for them, and re-layouts: 24.2 us -> 21.8 us
    pallas_call x7, Pallas kernels: 87.9 us -> 84 us  [exchange(): pl.pallas_call(functools.partial(exchange_kernel, tuple(plans)), out_shap...]
    gather x5 -> x0, local copies, waits for them, and re-layouts: 3.09 us -> none  [the longest x2 1.23 us: shards(): row_limit = jnp.repeat(limit[mine], BLOCK, total_repeat_length=row_total)]
where the time goes in v3:
time: 142 us
  Pallas kernels  84 us (59%)
  local copies, waits for them, and re-layouts  21.8 us (15%)
  matrix products  17.6 us (12%)
  other arithmetic  16.8 us (12%)
    pallas_call x7, Pallas kernels, exchange(): pl.pallas_call(functools.partial(exchange_kernel, tuple(plans)), out_shap...  84 us
    unnamed x80, local copies, waits for them, and re-layouts  7.81 us
    reshape x4, local copies, waits for them, and re-layouts, to_chunks(): return values.reshape(rows, pieces, width // pieces).transpose(1, 0, 2)  4.03 us
    dot_general x3, matrix products, contract_first(): lax.dot_general(left, right, (((0,), (0,)), ((), ())), preferred_element_...  3.92 us
    dot_general x6, matrix products, contract_last(): lax.dot_general(left, right, (((1,), (1,)), ((), ())), preferred_element_...  3.74 us
    reduce_sum x5, other arithmetic, total(): return jnp.sum(values.astype(jnp.float32), axis=0)  3.57 us
    gather x2, local copies, waits for them, and re-layouts, to_slots(): placed = held[source // slot_count, :, source % slot_count]  3.52 us
    dot_general x1, matrix products, shards(): up_pre = jnp.dot(n_one_b, gate_up[1], preferred_element_type=f32)  2.9 us

profile of v3, /device:TPU:0, one launch (start us, length us, event | category | flops | bytes accessed | tf_op | source)
XLA Modules:
  0.0 141.6 jit_solution(13541612926132529688)
XLA Ops:
  0.6 1.1 copy.117.refs_0_
  1.8 1.0 copy.118.refs_1_
  2.8 0.7 pad_maximum_fusion.refs_2_
  3.6 16.4 %shard_map.171 = (bf16[4,256,224]{2,1,0:T(8,128)(2,1)}, bf16[4,256,224]{2,1,0:T(8,128)(2,1)}, bf16[8,2,2,16,224]{4,3,2,1,0:T(8,128)(2,1)}) custom-call(bf16[256,224]{1,0:T(8,128)(2,1)} %copy-done.4, bf16[256,224]{1,0:T(8,128)(2,1)} %copy-done.7, bf16[8,2,2,16,224]{4,3,2,1,0:T(8,128)(2,1)} %pad_maximum_fusion.refs_2_), custom_call_target="tpu_custom_call" | custom-call | tf_op jit(solution)/shard_map/pallas_call | solution.py:224
  20.0 1.2 fusion.15
  21.2 1.2 fusion.26
  22.6 1.9 %fusion.9 = f32[256,640]{1,0:T(8,128)S(1)} fusion(bf16[256,896]{0,1:T(8,128)(2,1)S(1)} %bitcast.232, bf16[2,896,640]{2,1,0:T(8,128)(2,1)} %param.22), kind=kOutput, calls=%fused_computation.25 | convolution fusion | flops 293601280 | bytes 2260992 | tf_op jit(solution)/shard_map/dot_general | solution.py:360
  25.4 2.9 %add_reduce_fusion = (f32[256]{0:T(256)}, f32[256,640]{1,0:T(8,128)S(1)}) fusion(f32[256,640]{1,0:T(8,128)S(1)} %fusion.9, f32[256,640]{1,0:T(8,128)S(1)} %fusion.63, bf16[256,896]{0,1:T(8,128)(2,1)S(1)} %bitcast.233, bf16[2,896,640]{2,1,0:T(8,128)(2,1)} %param.22), kind=kOutput, calls=%fused_computation.47 | convolution fusion | flops 296713984 | bytes 3572736 | tf_op jit(solution)/shard_map/dot_general | solution.py:361
  28.3 0.9 copy-done.35
  29.2 0.7 fusion.7
  30.7 1.0 copy.124
  31.7 1.7 %convolution_convert_fusion = bf16[256,896]{1,0:T(8,128)(2,1)S(1)} fusion(bf16[640,896]{1,0:T(8,128)(2,1)S(1)} %copy-done, f32[256,640]{1,0:T(8,128)} %copy-done.35, f32[256,640]{1,0:T(8,128)S(1)} %fusion.9), kind=kOutput, calls=%fused_computation.11 | convolution fusion | flops 294813696 | bytes 2916352 | tf_op jit(solution)/shard_map/dot_general | solution.py:365
  33.6 1.0 copy.121
  34.8 1.3 gather_fusion
  36.1 12.6 %shard_map.172 = (f32[256,224]{1,0:T(8,128)}, f32[256,224]{1,0:T(8,128)}, f32[4,2,128]{2,1,0:T(2,128)}, bf16[8,2,2,16,224]{4,3,2,1,0:T(8,128)(2,1)}) custom-call(bf16[4,256,224]{2,1,0:T(8,128)(2,1)} %bitcast.203, bf16[4,256,224]{2,1,0:T(8,128)(2,1)} %bitcast.202, f32[2,128]{1,0:T(2,128)} %bitcast.243, bf16[8,2,2,16,224]{4,3,2,1,0:T(8,128)(2,1)} %bitcast.221), custom_call_target="tpu_custom_call" | custom-call | tf_op jit(solution)/shard_map/pallas_call | solution.py:224
  48.7 0.7 reduce_sum.211
  49.6 1.1 add_convert_fusion
  50.9 0.7 pad_maximum_fusion.1.refs_0_
  51.7 0.7 pad_maximum_fusion.2.refs_1_
  52.4 9.4 %shard_map.173 = (bf16[8,2,2,16,224]{4,3,2,1,0:T(8,128)(2,1)}, bf16[4,224,128]{2,1,0:T(8,128)(2,1)}) custom-call(bf16[8,2,2,16,224]{4,3,2,1,0:T(8,128)(2,1)} %pad_maximum_fusion.1.refs_0_, bf16[4,224,128]{2,1,0:T(8,128)(2,1)} %pad_maximum_fusion.2.refs_1_), custom_call_target="tpu_custom_call" | custom-call | tf_op jit(solution)/shard_map/pallas_call | solution.py:224
  61.8 2.2 %gather_fusion.1 = bf16[16,2,16,224]{3,2,1,0:T(8,128)(2,1)} fusion(bf16[8,2,2,16,224]{4,3,2,1,0:T(8,128)(2,1)} %get-tuple-element.31, s32[16]{0:T(128)S(1)} %fusion.50), kind=kCustom, calls=%fused_computation.1 | custom fusion | bytes 458880 | tf_op jit(solution)/shard_map/gather | solution.py:333
  64.0 9.8 %shard_map.174 = bf16[8,2,2,16,224]{4,3,2,1,0:T(8,128)(2,1)} custom-call(bf16[8,2,2,16,224]{4,3,2,1,0:T(8,128)(2,1)} %bitcast.220), custom_call_target="tpu_custom_call" | custom-call | tf_op jit(solution)/shard_map/pallas_call | solution.py:224
  73.8 1.0 fusion.58
  74.8 0.7 copy.131
  75.5 0.7 copy.132
  76.2 10.4 %shard_map.175 = (bf16[4,256,224]{2,1,0:T(8,128)(2,1)}, bf16[4,256,224]{2,1,0:T(8,128)(2,1)}) custom-call(bf16[256,224]{1,0:T(8,128)(2,1)} %bitcast.205, bf16[256,224]{1,0:T(8,128)(2,1)} %bitcast.214), custom_call_target="tpu_custom_call" | custom-call | tf_op jit(solution)/shard_map/pallas_call | solution.py:224
  86.6 1.1 convert_bitcast_fusion
  87.7 1.3 copy.134
  89.2 1.3 fusion.23
  90.5 0.9 fusion.61
  91.6 1.0 fusion.60
  95.1 1.0 copy.146
  96.1 2.0 %convolution_convert_fusion.2 = bf16[896,128]{1,0:T(8,128)(2,1)} fusion(bf16[256,896]{0,1:T(8,128)(2,1)} %bitcast.212, bf16[256,128]{0,1:T(8,128)(2,1)S(1)} %bitcast.235), kind=kOutput, calls=%fused_computation.16 | convolution fusion | flops 58834944 | bytes 753664 | tf_op jit(solution)/shard_map/dot_general | solution.py:271
  98.3 0.7 bitcast_multiply_fusion.1
  99.0 1.2 convolution_convert_fusion.5
  100.6 0.7 copy-done.22
  102.0 1.0 convolution_convert_fusion.3
  103.1 1.0 convolution_convert_fusion.4
  105.6 1.0 copy.143
  107.1 1.0 copy.137
  108.2 20.0 %shard_map.176 = (f32[256,224]{1,0:T(8,128)}, f32[256,224]{1,0:T(8,128)}, f32[4,2,128]{2,1,0:T(2,128)}, bf16[4,112,128]{2,1,0:T(8,128)(2,1)}, bf16[4,112,128]{2,...) custom-call(bf16[4,256,224]{2,1,0:T(8,128)(2,1)} %bitcast.201, bf16[4,256,224]{2,1,0:T(8,128)(2,1)} %bitcast.200, ...), custom_call_target="tpu_custom_call" | custom-call | tf_op jit(solution)/shard_map/pallas_call | solution.py:224
  128.1 1.5 %reduce_sum.226.refs_0_ = bf16[112,128]{1,0:T(8,128)(2,1)} reduce(bf16[4,112,128]{2,1,0:T(8,128)(2,1)} %get-tuple-element.39, bf16[]{:T(256)} %constant.91.clone.1), dimensions={0}, to_apply=%region_21.22 | reduce | flops 43008 | bytes 143362 | tf_op jit(solution)/shard_map/reduce_sum | solution.py:287
  129.7 5.5 %shard_map.177 = bf16[4,112,128]{2,1,0:T(8,128)(2,1)} custom-call(bf16[112,128]{1,0:T(8,128)(2,1)} %reduce_sum.226.refs_0_), custom_call_target="tpu_custom_call" | custom-call | tf_op jit(solution)/shard_map/pallas_call | solution.py:224
  135.2 1.0 convert_element_type.268
  137.1 0.8 copy.151
  138.0 0.8 copy.148
  140.1 0.7 copy.149
  140.8 0.8 copy.150
  (134 shorter events, 11.2 us)
Async XLA Ops:
  0.6 24.1 %copy-start = (bf16[640,896]{1,0:T(8,128)(2,1)S(1)}, bf16[640,896]{1,0:T(8,128)(2,1)}, u32[]{:S(2)}) copy-start(bf16[640,896]{1,0:T(8,128)(2,1)} %param.23) | copy-start | bytes 3440644
  1.7 1.8 %copy-start.4 = (bf16[256,224]{1,0:T(8,128)(2,1)}, bf16[256,224]{1,0:T(8,128)(2,1)S(1)}, u32[]{:S(2)}) copy-start(bf16[256,224]{1,0:T(8,128)(2,1)S(1)} %copy.117.refs_0_) | copy-start | bytes 344068
  2.8 0.8 copy-start.7
  22.6 1.9 %copy-start.13 = (bf16[4,256,224]{2,1,0:T(8,128)(2,1)S(1)}, bf16[4,256,224]{2,1,0:T(8,128)(2,1)}, u32[]{:S(2)}) copy-start(bf16[4,256,224]{2,1,0:T(8,128)(2,1)} %get-tuple-element.25) | copy-start | bytes 1376260
  25.4 3.8 %copy-start.34 = (bf16[2,896,640]{2,1,0:T(8,128)(2,1)S(1)}, bf16[2,896,640]{2,1,0:T(8,128)(2,1)}, u32[]{:S(2)}) copy-start(bf16[2,896,640]{2,1,0:T(8,128)(2,1)} %param.22) | copy-start | bytes 6881284
  28.3 0.9 copy-start.35
  33.4 1.2 copy-start.33
  33.4 1.4 copy-start.19
  34.6 14.8 %copy-start.25 = (bf16[256,224]{0,1:T(8,128)(2,1)S(1)}, bf16[256,224]{0,1:T(8,128)(2,1)}, u32[]{:S(2)}) copy-start(bf16[256,224]{0,1:T(8,128)(2,1)} %param.14) | copy-start | bytes 344068
  34.6 14.9 %copy-start.5 = (bf16[256,224]{1,0:T(8,128)(2,1)S(1)}, bf16[256,224]{1,0:T(8,128)(2,1)}, u32[]{:S(2)}) copy-start(bf16[256,224]{1,0:T(8,128)(2,1)} %copy-done.4) | copy-start | bytes 344068
  36.1 14.7 %copy-start.26 = (bf16[256,224]{0,1:T(8,128)(2,1)S(1)}, bf16[256,224]{0,1:T(8,128)(2,1)}, u32[]{:S(2)}) copy-start(bf16[256,224]{0,1:T(8,128)(2,1)} %param.13) | copy-start | bytes 344068
  48.7 2.2 %copy-start.20 = (f32[256,224]{1,0:T(8,128)S(1)}, f32[256,224]{1,0:T(8,128)}, u32[]{:S(2)}) copy-start(f32[256,224]{1,0:T(8,128)} %get-tuple-element.28) | copy-start | bytes 688132
  49.6 2.1 %copy-start.15 = (bf16[2,224,128]{2,1,0:T(8,128)(2,1)S(1)}, bf16[2,224,128]{2,1,0:T(8,128)(2,1)}, u32[]{:S(2)}) copy-start(bf16[2,224,128]{2,1,0:T(8,128)(2,1)} %param.20) | copy-start | bytes 344068
  87.7 1.3 copy-start.1
  89.0 1.5 %copy-start.8 = (bf16[896,128]{1,0:T(8,128)(2,1)S(1)}, bf16[896,128]{1,0:T(8,128)(2,1)}, u32[]{:S(2)}) copy-start(bf16[896,128]{1,0:T(8,128)(2,1)} %param.19) | copy-start | bytes 688132
  90.5 1.1 copy-start.10
  91.4 2.4 %copy-start.21 = (bf16[256,128]{0,1:T(8,128)(2,1)}, bf16[256,128]{0,1:T(8,128)(2,1)S(1)}, u32[]{:S(2)}) copy-start(bf16[256,128]{0,1:T(8,128)(2,1)S(1)} %get-tuple-element.88) | copy-start | bytes 196612
  91.4 1.1 copy-start.31
  91.4 1.4 %copy-start.32 = (s32[12]{0:T(128)S(1)}, s32[12]{0:T(128)}, u32[]{:S(2)}) copy-start(s32[12]{0:T(128)} %param.17) | copy-start | bytes 148
  92.5 1.7 %copy-start.23 = (bf16[256,128]{0,1:T(8,128)(2,1)}, bf16[256,128]{0,1:T(8,128)(2,1)S(1)}, u32[]{:S(2)}) copy-start(bf16[256,128]{0,1:T(8,128)(2,1)S(1)} %get-tuple-element.86) | copy-start | bytes 196612
  94.0 1.0 copy-start.2
  94.2 0.5 copy-start.30
  98.1 2.1 %copy-start.24 = (bf16[256,128]{0,1:T(8,128)(2,1)S(1)}, bf16[256,128]{0,1:T(8,128)(2,1)}, u32[]{:S(2)}) copy-start(bf16[256,128]{0,1:T(8,128)(2,1)} %copy-done.23) | copy-start | bytes 196612
  100.4 0.8 copy-start.22
  102.0 2.1 %copy-start.14 = (f32[256,128]{0,1:T(8,128)S(1)}, f32[256,128]{0,1:T(8,128)}, u32[]{:S(2)}) copy-start(f32[256,128]{0,1:T(8,128)} %get-tuple-element.87) | copy-start | bytes 393220
  102.0 2.2 %copy-start.12 = (f32[256,128]{0,1:T(8,128)S(1)}, f32[256,128]{0,1:T(8,128)}, u32[]{:S(2)}) copy-start(f32[256,128]{0,1:T(8,128)} %get-tuple-element.89) | copy-start | bytes 393220
  103.1 1.9 %copy-start.11 = (bf16[4,224,128]{2,1,0:T(8,128)(2,1)S(1)}, bf16[4,224,128]{2,1,0:T(8,128)(2,1)}, u32[]{:S(2)}) copy-start(bf16[4,224,128]{2,1,0:T(8,128)(2,1)} %get-tuple-element.33) | copy-start | bytes 688132
  105.4 1.2 copy-start.9
  108.2 28.7 %copy-start.16 = (bf16[8,2,2,16,224]{4,3,2,1,0:T(8,128)(2,1)S(1)}, bf16[8,2,2,16,224]{4,3,2,1,0:T(8,128)(2,1)}, u32[]{:S(2)}) copy-start(bf16[8,2,2,16,224]{4,3,2,1,0:T(8,128)(2,1)} %get-tuple-element.27) | copy-start | bytes 688132
  128.1 8.7 %copy-start.29 = (f32[4,2,128]{2,1,0:T(2,128)S(1)}, f32[4,2,128]{2,1,0:T(2,128)}, u32[]{:S(2)}) copy-start(f32[4,2,128]{2,1,0:T(2,128)} %get-tuple-element.37) | copy-start | bytes 12292
  135.1 1.8 %copy-start.3 = (bf16[1,2,8,16,224]{4,3,2,1,0:T(8,128)(2,1)S(1)}, bf16[1,2,8,16,224]{4,3,2,1,0:T(8,128)(2,1)}, u32[]{:S(2)}) copy-start(bf16[1,2,8,16,224]{4,3,2,1,0:T(8,128)(2,1)} %copy.131) | copy-start | bytes 344068
  135.2 1.8 %copy-start.18 = (f32[256,224]{1,0:T(8,128)S(1)}, f32[256,224]{1,0:T(8,128)}, u32[]{:S(2)}) copy-start(f32[256,224]{1,0:T(8,128)} %get-tuple-element.36) | copy-start | bytes 688132
  136.9 1.0 copy-start.17
  136.9 1.8 %copy-start.28 = (bf16[4,112,128]{2,1,0:T(8,128)(2,1)S(1)}, bf16[4,112,128]{2,1,0:T(8,128)(2,1)}, u32[]{:S(2)}) copy-start(bf16[4,112,128]{2,1,0:T(8,128)(2,1)} %get-tuple-element.40) | copy-start | bytes 344068
  137.0 2.5 %copy-start.27 = (bf16[4,112,128]{2,1,0:T(8,128)(2,1)S(1)}, bf16[4,112,128]{2,1,0:T(8,128)(2,1)}, u32[]{:S(2)}) copy-start(bf16[4,112,128]{2,1,0:T(8,128)(2,1)} %get-tuple-element.38) | copy-start | bytes 344068
  137.1 3.7 %copy-start.6 = (bf16[1,2,8,16,224]{4,3,2,1,0:T(8,128)(2,1)S(1)}, bf16[1,2,8,16,224]{4,3,2,1,0:T(8,128)(2,1)}, u32[]{:S(2)}) copy-start(bf16[1,2,8,16,224]{4,3,2,1,0:T(8,128)(2,1)} %copy.132) | copy-start | bytes 344068

commit v4 on v3

--- a/solution.py
+++ b/solution.py
@@ -232,6 +232,83 @@
     return [total(r) if add else r for r, add in zip(results, summed)]
 
 
+def spread_kernel(size, source, target, send_sem, recv_sem, own_sem):
+    me = lax.axis_index("seq")
+    part = lax.axis_index("mp")
+    near, far = near_of(part), far_of(part)
+    barrier = pltpu.get_barrier_semaphore()
+    for axis, count in (("seq", size), ("mp", 4)):
+        mine = lax.axis_index(axis)
+
+        def greet(k):
+            pl.semaphore_signal(
+                barrier,
+                inc=1,
+                device_id={axis: lax.rem(mine + k, count)},
+                device_id_type=pl.DeviceIdType.MESH,
+            )
+
+        each(1, count, greet)
+    pl.semaphore_wait(barrier, size + 2)
+
+    def seq_copy(k):
+        peer = lax.rem(me + k, size)
+        return remote(
+            source.at[peer], target.at[part, me], send_sem.at[k], recv_sem.at[k], "seq", peer
+        )
+
+    def pass_copy(k, phase):
+        piece = lax.rem(me + size - k, size)
+        block = target.at[far if phase == 3 else part, piece]
+        place = phase * size + k
+        return remote(
+            block, block, send_sem.at[place], recv_sem.at[place], "mp", far if phase == 1 else near
+        )
+
+    def hand_on(k):
+        pass_copy(k, 1).wait_recv()
+        pass_copy(k, 3).start()
+
+    def arrive(k):
+        seq_copy(k).wait_recv()
+        pass_copy(k, 1).start()
+        pass_copy(k, 2).start()
+        hand_on(k - 1)
+
+    def finish(k):
+        pass_copy(k, 1).wait_send()
+        pass_copy(k, 2).wait()
+        pass_copy(k, 3).wait()
+
+    each(1, size, lambda k: seq_copy(k).start())
+    own = pltpu.make_async_copy(source.at[me], target.at[part, me], own_sem)
+    own.start()
+    own.wait()
+    pass_copy(0, 1).start()
+    pass_copy(0, 2).start()
+    each(1, size, arrive)
+    hand_on(size - 1)
+    each(0, size, finish)
+    each(1, size, lambda k: seq_copy(k).wait_send())
+
+
+def spread(number, placed):
+    size = lax.axis_size("seq")
+    if lax.axis_size("mp") != 4:
+        (owned,) = exchange(number, (placed, "seq", "send"))
+        return exchange(number + 10, (owned, "mp", "gather"))[0]
+    anywhere = pl.BlockSpec(memory_space=pl.ANY)
+    sems = pltpu.SemaphoreType.DMA((4 * size,))
+    return pl.pallas_call(
+        functools.partial(spread_kernel, size),
+        out_shape=jax.ShapeDtypeStruct((4,) + placed.shape, placed.dtype),
+        in_specs=[anywhere],
+        out_specs=anywhere,
+        scratch_shapes=[sems, sems, pltpu.SemaphoreType.DMA],
+        compiler_params=pltpu.CompilerParams(collective_id=number, has_side_effects=True),
+    )(placed)
+
+
 def normalize(values):
     inverse = lax.rsqrt(jnp.mean(values * values, axis=-1, keepdims=True) + EPSILON)
     return (values * inverse, inverse)
@@ -386,11 +463,11 @@
         2, (to_shares(second_pack, first_pack), "seq", "send"), (kv_sent, "mp", "send")
     )
     kv_local = kv_parts.reshape(width, 2 * head_size)
-    (owned,) = exchange(3, (to_slots(held), "seq", "send"))
+    everyone = spread(3, to_slots(held))
+    owned = lax.dynamic_index_in_dim(everyone, lax.axis_index("mp"), 0, keepdims=False)
     second_share, first_share = from_shares(owned)
-    second_all, cot_all = exchange(4, (second_share, "mp", "relay"), (first_share, "mp", "relay"))
-    second_in = from_chunks(second_all)
-    first_cot = from_chunks(cot_all)
+    whole = everyone.transpose(3, 2, 1, 4, 0, 5).reshape(2, row_total, width)
+    second_in, first_cot = whole[0], whole[1]
 
     n_two, r_two = normalize(second_in.astype(f32))
     n_two_b = n_two.astype(bf16)

time: 142 us -> 154 us (1.085)
  local copies, waits for them, and re-layouts: 21.8 us -> 28.4 us
  matrix products: 17.6 us -> 21 us
    pallas_call x0 -> x1, Pallas kernels: none -> 22.5 us  [spread(): pl.pallas_call(functools.partial(spread_kernel, size), out_shape=jax.Shap...]
    pallas_call x7 -> x5, Pallas kernels: 84 us -> 62.8 us  [exchange(): pl.pallas_call(functools.partial(exchange_kernel, tuple(plans)), out_shap...]
    mul x1 -> x2, local copies, waits for them, and re-layouts: 0.99 us -> 3.42 us  [shards(): masked_cot = first_cot * live.astype(bf16)]
    slice x0 -> x1, local copies, waits for them, and re-layouts: none -> 2.41 us  [shards(): second_in, first_cot = (whole[0], whole[1])]
    another operation x3, local copies, waits for them, and re-layouts: 2.32 us -> 0.04 us  [shards(): second_share, first_share = from_shares(owned)]
    squeeze x0 -> x1, local copies, waits for them, and re-layouts: none -> 2.23 us  [shards(): second_in, first_cot = (whole[0], whole[1])]
    unnamed x80 -> x74, local copies, waits for them, and re-layouts: 7.81 us -> 7.42 us
where the time goes in v4:
time: 154 us; the launch traced here: 153 us
  Pallas kernels  85.3 us (55%)
  local copies, waits for them, and re-layouts  28.4 us (18%)
  matrix products  21 us (14%)
  other arithmetic  17.1 us (11%)
    pallas_call x5, Pallas kernels, exchange(): pl.pallas_call(functools.partial(exchange_kernel, tuple(plans)), out_shap...  62.8 us
    pallas_call x1, Pallas kernels, spread(): pl.pallas_call(functools.partial(spread_kernel, size), out_shape=jax.Shap...  22.5 us
    unnamed x74, local copies, waits for them, and re-layouts  7.42 us
    dot_general x3, matrix products, contract_first(): lax.dot_general(left, right, (((0,), (0,)), ((), ())), preferred_element_...  4.12 us
    reshape x4, local copies, waits for them, and re-layouts, to_chunks(): return values.reshape(rows, pieces, width // pieces).transpose(1, 0, 2)  4.01 us
    dot_general x6, matrix products, contract_last(): lax.dot_general(left, right, (((1,), (1,)), ((), ())), preferred_element_...  3.98 us
    reduce_sum x5, other arithmetic, total(): return jnp.sum(values.astype(jnp.float32), axis=0)  3.57 us
    gather x2, local copies, waits for them, and re-layouts, to_slots(): placed = held[source // slot_count, :, source % slot_count]  3.52 us

profile of v4, /device:TPU:0, one launch (start us, length us, event | category | flops | bytes accessed | tf_op | source)
XLA Modules:
  0.0 153.1 jit_solution(13733498376397532045)
XLA Ops:
  0.6 1.1 copy.152.refs_0_
  1.8 1.0 copy.153.refs_1_
  2.8 0.7 pad_maximum_fusion.refs_2_
  3.6 16.4 %shard_map.171 = (bf16[4,256,224]{2,1,0:T(8,128)(2,1)}, bf16[4,256,224]{2,1,0:T(8,128)(2,1)}, bf16[8,2,2,16,224]{4,3,2,1,0:T(8,128)(2,1)}) custom-call(bf16[256,224]{1,0:T(8,128)(2,1)} %copy-done.3, bf16[256,224]{1,0:T(8,128)(2,1)} %copy-done.5, bf16[8,2,2,16,224]{4,3,2,1,0:T(8,128)(2,1)} %pad_maximum_fusion.refs_2_), custom_call_target="tpu_custom_call" | custom-call | tf_op jit(solution)/shard_map/pallas_call | solution.py:224
  20.0 1.2 fusion.15
  21.2 1.2 fusion.22
  22.6 1.9 %fusion.9 = f32[256,640]{1,0:T(8,128)S(1)} fusion(bf16[256,896]{0,1:T(8,128)(2,1)S(1)} %bitcast.215, bf16[2,896,640]{2,1,0:T(8,128)(2,1)} %param.22), kind=kOutput, calls=%fused_computation.22 | convolution fusion | flops 293601280 | bytes 2260992 | tf_op jit(solution)/shard_map/dot_general | solution.py:437
  25.4 2.9 %add_reduce_fusion = (f32[256]{0:T(256)}, f32[256,640]{1,0:T(8,128)S(1)}) fusion(f32[256,640]{1,0:T(8,128)S(1)} %fusion.9, f32[256,640]{1,0:T(8,128)S(1)} %fusion.65, bf16[256,896]{0,1:T(8,128)(2,1)S(1)} %bitcast.216, bf16[2,896,640]{2,1,0:T(8,128)(2,1)} %param.22), kind=kOutput, calls=%fused_computation.42 | convolution fusion | flops 296713984 | bytes 3572736 | tf_op jit(solution)/shard_map/dot_general | solution.py:438
  30.0 1.0 copy.159
  31.0 1.7 %convolution_convert_fusion = bf16[256,896]{1,0:T(8,128)(2,1)S(1)} fusion(bf16[640,896]{1,0:T(8,128)(2,1)S(1)} %copy-done, f32[256,640]{1,0:T(8,128)} %copy-done.32, f32[256,640]{1,0:T(8,128)S(1)} %fusion.9), kind=kOutput, calls=%fused_computation.8 | convolution fusion | flops 294813696 | bytes 2916352 | tf_op jit(solution)/shard_map/dot_general | solution.py:442
  32.9 1.0 copy.156
  34.0 1.3 gather_fusion
  35.3 12.7 %shard_map.172 = (f32[256,224]{1,0:T(8,128)}, f32[256,224]{1,0:T(8,128)}, f32[4,2,128]{2,1,0:T(2,128)}, bf16[8,2,2,16,224]{4,3,2,1,0:T(8,128)(2,1)}) custom-call(bf16[4,256,224]{2,1,0:T(8,128)(2,1)} %bitcast.190, bf16[4,256,224]{2,1,0:T(8,128)(2,1)} %bitcast.189, f32[2,128]{1,0:T(2,128)} %bitcast.224, bf16[8,2,2,16,224]{4,3,2,1,0:T(8,128)(2,1)} %bitcast.202), custom_call_target="tpu_custom_call" | custom-call | tf_op jit(solution)/shard_map/pallas_call | solution.py:224
  48.0 0.7 reduce_sum.211
  48.8 1.1 add_convert_fusion
  50.2 0.7 pad_maximum_fusion.1.refs_0_
  50.9 0.7 pad_maximum_fusion.2.refs_1_
  51.7 9.4 %shard_map.173 = (bf16[8,2,2,16,224]{4,3,2,1,0:T(8,128)(2,1)}, bf16[4,224,128]{2,1,0:T(8,128)(2,1)}) custom-call(bf16[8,2,2,16,224]{4,3,2,1,0:T(8,128)(2,1)} %pad_maximum_fusion.1.refs_0_, bf16[4,224,128]{2,1,0:T(8,128)(2,1)} %pad_maximum_fusion.2.refs_1_), custom_call_target="tpu_custom_call" | custom-call | tf_op jit(solution)/shard_map/pallas_call | solution.py:224
  61.0 2.3 %gather_fusion.1 = bf16[16,2,16,224]{3,2,1,0:T(8,128)(2,1)} fusion(bf16[8,2,2,16,224]{4,3,2,1,0:T(8,128)(2,1)} %get-tuple-element.29, s32[16]{0:T(128)S(1)} %fusion.52), kind=kCustom, calls=%fused_computation.1 | custom fusion | bytes 458880 | tf_op jit(solution)/shard_map/gather | solution.py:410
  63.3 22.5 %shard_map.174 = bf16[4,8,2,2,16,224]{5,4,3,2,1,0:T(8,128)(2,1)} custom-call(bf16[8,2,2,16,224]{4,3,2,1,0:T(8,128)(2,1)} %bitcast.199), custom_call_target="tpu_custom_call" | custom-call | tf_op jit(solution)/shard_map/pallas_call | solution.py:302
  86.4 0.7 fusion.45
  87.1 2.2 %broadcast_multiply_fusion = (bf16[1,2,8,16,4,224]{5,3,0,1,2,4:T(8,128)(2,1)}, bf16[1,2,8,16,4,224]{5,3,0,1,2,4:T(8,128)(2,1)}, f32[1,2,8,16,4,224]{5,3,0,1,2,4:T(8,128)S(1)}) fusion(bf16[2,8,16]{2,0,1:T(2,128)(2,1)S(1)} %compare_convert_fusion, bf16[2,2,8,16,4,224]{5,3,0,1,2,4:T(8,128)(2,1)} %bitcast.184), kind=kLoop, calls=%fused_computation.68 | loop fusion | flops 458752 | bytes 2753024 | tf_op jit(solution)/shard_map/mul | solution.py:502
  89.4 0.7 copy.169
  90.1 1.6 %reshape.583 = f32[256,896]{1,0:T(8,128)} reshape(f32[1,2,8,16,4,224]{5,4,3,2,1,0:T(4,128)S(1)} %copy.169) | data formatting | bytes 1835008 | tf_op jit(solution)/shard_map/convert_element_type | solution.py:472
  92.0 2.2 %fusion.63 = (bf16[256,128]{0,1:T(8,128)(2,1)}, f32[256,128]{0,1:T(8,128)}) fusion(bf16[896,128]{1,0:T(8,128)(2,1)S(1)} %copy-done.7, f32[256,896]{1,0:T(8,128)} %reshape.583, f32[256]{0:T(256)S(1)} %rsqrt.22), kind=kOutput, calls=%fused_computation.149 | convolution fusion | flops 59211776 | bytes 1344512 | tf_op jit(solution)/shard_map/dot_general | solution.py:474
  95.8 0.7 broadcast_bitcast_fusion
  96.6 1.1 fusion.64
  97.9 0.9 convolution_convert_fusion.9
  98.9 1.2 copy.179
  100.1 2.2 %mul.239 = bf16[256,896]{1,0:T(8,128)(2,1)} reshape(bf16[1,2,8,16,4,224]{5,4,3,2,1,0:T(4,128)(2,1)} %copy.179) | data formatting | bytes 917504 | tf_op jit(solution)/shard_map/mul | solution.py:502
  102.3 2.0 %convolution_convert_fusion.2 = bf16[896,128]{1,0:T(8,128)(2,1)} fusion(bf16[256,896]{1,0:T(8,128)(2,1)} %mul.239, bf16[256,128]{0,1:T(8,128)(2,1)} %bitcast.218), kind=kOutput, calls=%fused_computation.13 | convolution fusion | flops 58834944 | bytes 753664 | tf_op jit(solution)/shard_map/dot_general | solution.py:348
  104.4 2.4 %copy.173 = bf16[1,2,8,16,4,224]{5,4,3,2,1,0:T(4,128)(2,1)} copy(bf16[1,2,8,16,4,224]{5,3,0,1,2,4:T(8,128)(2,1)} %get-tuple-element.80) | data formatting | bytes 917504 | tf_op jit(solution)/shard_map/slice | solution.py:470
  106.8 2.2 %squeeze.22 = bf16[256,896]{1,0:T(8,128)(2,1)} reshape(bf16[1,2,8,16,4,224]{5,4,3,2,1,0:T(4,128)(2,1)} %copy.173) | data formatting | bytes 917504 | tf_op jit(solution)/shard_map/squeeze | solution.py:470
  109.7 1.4 convolution_convert_fusion.5
  111.1 1.0 multiply_reduce_fusion.1
  113.5 1.0 convolution_convert_fusion.3
  114.7 1.0 convolution_convert_fusion.4
  117.2 1.0 copy.178
  118.8 1.0 copy.172
  119.8 19.0 %shard_map.175 = (f32[256,224]{1,0:T(8,128)}, f32[256,224]{1,0:T(8,128)}, f32[4,2,128]{2,1,0:T(2,128)}, bf16[4,112,128]{2,1,0:T(8,128)(2,1)}, bf16[4,112,128]{2,...) custom-call(bf16[4,256,224]{2,1,0:T(8,128)(2,1)} %bitcast.188, bf16[4,256,224]{2,1,0:T(8,128)(2,1)} %bitcast.187, ...), custom_call_target="tpu_custom_call" | custom-call | tf_op jit(solution)/shard_map/pallas_call | solution.py:224
  138.8 1.5 %reduce_sum.226.refs_0_ = bf16[112,128]{1,0:T(8,128)(2,1)} reduce(bf16[4,112,128]{2,1,0:T(8,128)(2,1)} %get-tuple-element.35, bf16[]{:T(256)} %constant.102.clone.1), dimensions={0}, to_apply=%region_21.22 | reduce | flops 43008 | bytes 143362 | tf_op jit(solution)/shard_map/reduce_sum | solution.py:364
  140.3 5.5 %shard_map.176 = bf16[4,112,128]{2,1,0:T(8,128)(2,1)} custom-call(bf16[112,128]{1,0:T(8,128)(2,1)} %reduce_sum.226.refs_0_), custom_call_target="tpu_custom_call" | custom-call | tf_op jit(solution)/shard_map/pallas_call | solution.py:224
  145.8 1.0 convert_element_type.263
  147.7 0.8 copy-done.14
  148.6 0.8 copy.186
  149.5 0.8 copy.183
  151.6 0.7 copy.184
  152.3 0.8 copy.185
  (132 shorter events, 12.7 us)
Async XLA Ops:
  0.6 24.1 %copy-start = (bf16[640,896]{1,0:T(8,128)(2,1)S(1)}, bf16[640,896]{1,0:T(8,128)(2,1)}, u32[]{:S(2)}) copy-start(bf16[640,896]{1,0:T(8,128)(2,1)} %param.23) | copy-start | bytes 3440644
  1.7 1.8 %copy-start.3 = (bf16[256,224]{1,0:T(8,128)(2,1)}, bf16[256,224]{1,0:T(8,128)(2,1)S(1)}, u32[]{:S(2)}) copy-start(bf16[256,224]{1,0:T(8,128)(2,1)S(1)} %copy.152.refs_0_) | copy-start | bytes 344068
  2.8 0.8 copy-start.5
  22.6 1.9 %copy-start.10 = (bf16[4,256,224]{2,1,0:T(8,128)(2,1)S(1)}, bf16[4,256,224]{2,1,0:T(8,128)(2,1)}, u32[]{:S(2)}) copy-start(bf16[4,256,224]{2,1,0:T(8,128)(2,1)} %get-tuple-element.23) | copy-start | bytes 1376260
  25.4 2.9 %copy-start.31 = (bf16[2,896,640]{2,1,0:T(8,128)(2,1)S(1)}, bf16[2,896,640]{2,1,0:T(8,128)(2,1)}, u32[]{:S(2)}) copy-start(bf16[2,896,640]{2,1,0:T(8,128)(2,1)} %param.22) | copy-start | bytes 6881284
  28.3 0.8 copy-start.32
  32.6 1.2 copy-start.30
  32.6 1.4 copy-start.16
  33.9 14.8 %copy-start.22 = (bf16[256,224]{0,1:T(8,128)(2,1)S(1)}, bf16[256,224]{0,1:T(8,128)(2,1)}, u32[]{:S(2)}) copy-start(bf16[256,224]{0,1:T(8,128)(2,1)} %param.14) | copy-start | bytes 344068
  33.9 14.9 %copy-start.4 = (bf16[256,224]{1,0:T(8,128)(2,1)S(1)}, bf16[256,224]{1,0:T(8,128)(2,1)}, u32[]{:S(2)}) copy-start(bf16[256,224]{1,0:T(8,128)(2,1)} %copy-done.3) | copy-start | bytes 344068
  35.3 14.7 %copy-start.23 = (bf16[256,224]{0,1:T(8,128)(2,1)S(1)}, bf16[256,224]{0,1:T(8,128)(2,1)}, u32[]{:S(2)}) copy-start(bf16[256,224]{0,1:T(8,128)(2,1)} %param.13) | copy-start | bytes 344068
  48.0 2.2 %copy-start.17 = (f32[256,224]{1,0:T(8,128)S(1)}, f32[256,224]{1,0:T(8,128)}, u32[]{:S(2)}) copy-start(f32[256,224]{1,0:T(8,128)} %get-tuple-element.26) | copy-start | bytes 688132
  48.8 2.1 %copy-start.11 = (bf16[2,224,128]{2,1,0:T(8,128)(2,1)S(1)}, bf16[2,224,128]{2,1,0:T(8,128)(2,1)}, u32[]{:S(2)}) copy-start(bf16[2,224,128]{2,1,0:T(8,128)(2,1)} %param.20) | copy-start | bytes 344068
  51.7 34.1 %copy-start.28 = (s32[12]{0:T(128)S(1)}, s32[12]{0:T(128)}, u32[]{:S(2)}) copy-start(s32[12]{0:T(128)} %param.16) | copy-start | bytes 148
  51.7 34.5 %copy-start.29 = (s32[12]{0:T(128)S(1)}, s32[12]{0:T(128)}, u32[]{:S(2)}) copy-start(s32[12]{0:T(128)} %param.17) | copy-start | bytes 148
  90.1 1.7 %copy-start.1 = (bf16[4,8,2,2,16,224]{5,4,3,2,1,0:T(8,128)(2,1)S(1)}, bf16[4,8,2,2,16,224]{5,4,3,2,1,0:T(8,128)(2,1)}, u32[]{:S(2)}) copy-start(bf16[4,8,2,2,16,224]{5,4,3,2,1,0:T(8,128)(2,1)} %shard_map.174) | copy-start | bytes 2752516
  90.1 2.0 %copy-start.7 = (bf16[896,128]{1,0:T(8,128)(2,1)S(1)}, bf16[896,128]{1,0:T(8,128)(2,1)}, u32[]{:S(2)}) copy-start(bf16[896,128]{1,0:T(8,128)(2,1)} %param.19) | copy-start | bytes 688132
  94.4 0.9 copy-start.6
  95.7 3.0 %copy-start.20 = (bf16[256,128]{0,1:T(8,128)(2,1)}, bf16[256,128]{0,1:T(8,128)(2,1)S(1)}, u32[]{:S(2)}) copy-start(bf16[256,128]{0,1:T(8,128)(2,1)S(1)} %get-tuple-element.92) | copy-start | bytes 196612
  95.8 2.0 %copy-start.27 = (pred[256]{0:T(512)(128)(4,1)}, pred[256]{0:T(512)(128)(4,1)S(1)}, u32[]{:S(2)}) copy-start(pred[256]{0:T(512)(128)(4,1)S(1)} %get-tuple-element.78) | copy-start | bytes 772
  97.9 1.0 copy-start.2
  112.1 0.8 copy-start.18
  113.2 1.3 copy-start.21
  113.4 2.3 %copy-start.9 = (f32[256,128]{0,1:T(8,128)S(1)}, f32[256,128]{0,1:T(8,128)}, u32[]{:S(2)}) copy-start(f32[256,128]{0,1:T(8,128)} %get-tuple-element.95) | copy-start | bytes 393220
  113.5 2.9 %copy-start.8 = (bf16[896,128]{1,0:T(8,128)(2,1)S(1)}, bf16[896,128]{1,0:T(8,128)(2,1)}, u32[]{:S(2)}) copy-start(bf16[896,128]{1,0:T(8,128)(2,1)} %param.19) | copy-start | bytes 688132
  117.0 1.3 copy-start.15
  117.0 1.3 copy-start.19
  138.8 8.7 %copy-start.26 = (f32[4,2,128]{2,1,0:T(2,128)S(1)}, f32[4,2,128]{2,1,0:T(2,128)}, u32[]{:S(2)}) copy-start(f32[4,2,128]{2,1,0:T(2,128)} %get-tuple-element.33) | copy-start | bytes 12292
  145.8 1.8 %copy-start.12 = (bf16[8,2,2,16,224]{4,3,2,1,0:T(8,128)(2,1)S(1)}, bf16[8,2,2,16,224]{4,3,2,1,0:T(8,128)(2,1)}, u32[]{:S(2)}) copy-start(bf16[8,2,2,16,224]{4,3,2,1,0:T(8,128)(2,1)} %get-tuple-element.25) | copy-start | bytes 688132
  147.5 1.0 copy-start.14
  147.6 1.8 %copy-start.13 = (f32[256,224]{1,0:T(8,128)S(1)}, f32[256,224]{1,0:T(8,128)}, u32[]{:S(2)}) copy-start(f32[256,224]{1,0:T(8,128)} %get-tuple-element.31) | copy-start | bytes 688132
  148.5 1.8 %copy-start.25 = (bf16[4,112,128]{2,1,0:T(8,128)(2,1)S(1)}, bf16[4,112,128]{2,1,0:T(8,128)(2,1)}, u32[]{:S(2)}) copy-start(bf16[4,112,128]{2,1,0:T(8,128)(2,1)} %get-tuple-element.36) | copy-start | bytes 344068
  148.5 2.4 %copy-start.24 = (bf16[4,112,128]{2,1,0:T(8,128)(2,1)S(1)}, bf16[4,112,128]{2,1,0:T(8,128)(2,1)}, u32[]{:S(2)}) copy-start(bf16[4,112,128]{2,1,0:T(8,128)(2,1)} %get-tuple-element.34) | copy-start | bytes 344068

commit v5 on v3

--- a/solution.py
+++ b/solution.py
@@ -467,7 +467,7 @@
     second_cot = (
         cot_second_own.astype(f32) + (norm_two_share - n_two_share * inner_two) * r_two
     ).astype(bf16)
-    (kv_all,) = exchange(6, (total(kv_got).astype(bf16), "mp", "relay"))
+    (kv_all,) = exchange(6, (total(kv_got).astype(bf16), "mp", "gather"))
     kv_all = kv_all.astype(f32)
     kv_share = jnp.stack(
         [

time: 142 us -> 141 us (level)
  no operation moved by 1% of the time
where the time goes in v5:
time: 141 us; the launch traced here: 140 us
  Pallas kernels  82.8 us (59%)
  local copies, waits for them, and re-layouts  21.8 us (15%)
  matrix products  17.6 us (12%)
  other arithmetic  16.8 us (12%)
    pallas_call x7, Pallas kernels, exchange(): pl.pallas_call(functools.partial(exchange_kernel, tuple(plans)), out_shap...  82.8 us
    unnamed x80, local copies, waits for them, and re-layouts  7.81 us
    reshape x4, local copies, waits for them, and re-layouts, to_chunks(): return values.reshape(rows, pieces, width // pieces).transpose(1, 0, 2)  4.03 us
    dot_general x3, matrix products, contract_first(): lax.dot_general(left, right, (((0,), (0,)), ((), ())), preferred_element_...  3.92 us
    dot_general x6, matrix products, contract_last(): lax.dot_general(left, right, (((1,), (1,)), ((), ())), preferred_element_...  3.74 us
    reduce_sum x5, other arithmetic, total(): return jnp.sum(values.astype(jnp.float32), axis=0)  3.57 us
    gather x2, local copies, waits for them, and re-layouts, to_slots(): placed = held[source // slot_count, :, source % slot_count]  3.52 us
    dot_general x1, matrix products, shards(): up_pre = jnp.dot(n_one_b, gate_up[1], preferred_element_type=f32)  2.9 us

profile of v5, /device:TPU:0, one launch (start us, length us, event | category | flops | bytes accessed | tf_op | source)
XLA Modules:
  0.0 140.4 jit_solution(2378871169853533835)
XLA Ops:
  0.6 1.1 copy.117.refs_0_
  1.8 1.0 copy.118.refs_1_
  2.8 0.7 pad_maximum_fusion.refs_2_
  3.6 16.4 %shard_map.171 = (bf16[4,256,224]{2,1,0:T(8,128)(2,1)}, bf16[4,256,224]{2,1,0:T(8,128)(2,1)}, bf16[8,2,2,16,224]{4,3,2,1,0:T(8,128)(2,1)}) custom-call(bf16[256,224]{1,0:T(8,128)(2,1)} %copy-done.4, bf16[256,224]{1,0:T(8,128)(2,1)} %copy-done.7, bf16[8,2,2,16,224]{4,3,2,1,0:T(8,128)(2,1)} %pad_maximum_fusion.refs_2_), custom_call_target="tpu_custom_call" | custom-call | tf_op jit(solution)/shard_map/pallas_call | solution.py:224
  20.0 1.2 fusion.15
  21.2 1.2 fusion.26
  22.6 1.9 %fusion.9 = f32[256,640]{1,0:T(8,128)S(1)} fusion(bf16[256,896]{0,1:T(8,128)(2,1)S(1)} %bitcast.232, bf16[2,896,640]{2,1,0:T(8,128)(2,1)} %param.22), kind=kOutput, calls=%fused_computation.25 | convolution fusion | flops 293601280 | bytes 2260992 | tf_op jit(solution)/shard_map/dot_general | solution.py:360
  25.4 2.9 %add_reduce_fusion = (f32[256]{0:T(256)}, f32[256,640]{1,0:T(8,128)S(1)}) fusion(f32[256,640]{1,0:T(8,128)S(1)} %fusion.9, f32[256,640]{1,0:T(8,128)S(1)} %fusion.63, bf16[256,896]{0,1:T(8,128)(2,1)S(1)} %bitcast.233, bf16[2,896,640]{2,1,0:T(8,128)(2,1)} %param.22), kind=kOutput, calls=%fused_computation.47 | convolution fusion | flops 296713984 | bytes 3572736 | tf_op jit(solution)/shard_map/dot_general | solution.py:361
  28.3 0.9 copy-done.35
  29.2 0.7 fusion.7
  30.7 1.0 copy.124
  31.7 1.7 %convolution_convert_fusion = bf16[256,896]{1,0:T(8,128)(2,1)S(1)} fusion(bf16[640,896]{1,0:T(8,128)(2,1)S(1)} %copy-done, f32[256,640]{1,0:T(8,128)} %copy-done.35, f32[256,640]{1,0:T(8,128)S(1)} %fusion.9), kind=kOutput, calls=%fused_computation.11 | convolution fusion | flops 294813696 | bytes 2916352 | tf_op jit(solution)/shard_map/dot_general | solution.py:365
  33.6 1.0 copy.121
  34.8 1.3 gather_fusion
  36.1 12.6 %shard_map.172 = (f32[256,224]{1,0:T(8,128)}, f32[256,224]{1,0:T(8,128)}, f32[4,2,128]{2,1,0:T(2,128)}, bf16[8,2,2,16,224]{4,3,2,1,0:T(8,128)(2,1)}) custom-call(bf16[4,256,224]{2,1,0:T(8,128)(2,1)} %bitcast.203, bf16[4,256,224]{2,1,0:T(8,128)(2,1)} %bitcast.202, f32[2,128]{1,0:T(2,128)} %bitcast.243, bf16[8,2,2,16,224]{4,3,2,1,0:T(8,128)(2,1)} %bitcast.221), custom_call_target="tpu_custom_call" | custom-call | tf_op jit(solution)/shard_map/pallas_call | solution.py:224
  48.7 0.7 reduce_sum.211
  49.6 1.1 add_convert_fusion
  50.9 0.7 pad_maximum_fusion.1.refs_0_
  51.7 0.7 pad_maximum_fusion.2.refs_1_
  52.4 9.4 %shard_map.173 = (bf16[8,2,2,16,224]{4,3,2,1,0:T(8,128)(2,1)}, bf16[4,224,128]{2,1,0:T(8,128)(2,1)}) custom-call(bf16[8,2,2,16,224]{4,3,2,1,0:T(8,128)(2,1)} %pad_maximum_fusion.1.refs_0_, bf16[4,224,128]{2,1,0:T(8,128)(2,1)} %pad_maximum_fusion.2.refs_1_), custom_call_target="tpu_custom_call" | custom-call | tf_op jit(solution)/shard_map/pallas_call | solution.py:224
  61.8 2.2 %gather_fusion.1 = bf16[16,2,16,224]{3,2,1,0:T(8,128)(2,1)} fusion(bf16[8,2,2,16,224]{4,3,2,1,0:T(8,128)(2,1)} %get-tuple-element.31, s32[16]{0:T(128)S(1)} %fusion.50), kind=kCustom, calls=%fused_computation.1 | custom fusion | bytes 458880 | tf_op jit(solution)/shard_map/gather | solution.py:333
  64.0 9.8 %shard_map.174 = bf16[8,2,2,16,224]{4,3,2,1,0:T(8,128)(2,1)} custom-call(bf16[8,2,2,16,224]{4,3,2,1,0:T(8,128)(2,1)} %bitcast.220), custom_call_target="tpu_custom_call" | custom-call | tf_op jit(solution)/shard_map/pallas_call | solution.py:224
  73.8 1.0 fusion.58
  74.8 0.7 copy.131
  75.5 0.7 copy.132
  76.2 10.4 %shard_map.175 = (bf16[4,256,224]{2,1,0:T(8,128)(2,1)}, bf16[4,256,224]{2,1,0:T(8,128)(2,1)}) custom-call(bf16[256,224]{1,0:T(8,128)(2,1)} %bitcast.205, bf16[256,224]{1,0:T(8,128)(2,1)} %bitcast.214), custom_call_target="tpu_custom_call" | custom-call | tf_op jit(solution)/shard_map/pallas_call | solution.py:224
  86.6 1.1 convert_bitcast_fusion
  87.7 1.3 copy.134
  89.2 1.3 fusion.23
  90.5 0.9 fusion.61
  91.6 1.0 fusion.60
  95.1 1.0 copy.146
  96.1 2.0 %convolution_convert_fusion.2 = bf16[896,128]{1,0:T(8,128)(2,1)} fusion(bf16[256,896]{0,1:T(8,128)(2,1)} %bitcast.212, bf16[256,128]{0,1:T(8,128)(2,1)S(1)} %bitcast.235), kind=kOutput, calls=%fused_computation.16 | convolution fusion | flops 58834944 | bytes 753664 | tf_op jit(solution)/shard_map/dot_general | solution.py:271
  98.3 0.7 bitcast_multiply_fusion.1
  99.0 1.2 convolution_convert_fusion.5
  100.6 0.7 copy-done.22
  102.0 1.0 convolution_convert_fusion.3
  103.1 1.0 convolution_convert_fusion.4
  105.6 1.0 copy.143
  107.1 1.0 copy.137
  108.2 20.0 %shard_map.176 = (f32[256,224]{1,0:T(8,128)}, f32[256,224]{1,0:T(8,128)}, f32[4,2,128]{2,1,0:T(2,128)}, bf16[4,112,128]{2,1,0:T(8,128)(2,1)}, bf16[4,112,128]{2,...) custom-call(bf16[4,256,224]{2,1,0:T(8,128)(2,1)} %bitcast.201, bf16[4,256,224]{2,1,0:T(8,128)(2,1)} %bitcast.200, ...), custom_call_target="tpu_custom_call" | custom-call | tf_op jit(solution)/shard_map/pallas_call | solution.py:224
  128.1 1.5 %reduce_sum.226.refs_0_ = bf16[112,128]{1,0:T(8,128)(2,1)} reduce(bf16[4,112,128]{2,1,0:T(8,128)(2,1)} %get-tuple-element.39, bf16[]{:T(256)} %constant.91.clone.1), dimensions={0}, to_apply=%region_21.22 | reduce | flops 43008 | bytes 143362 | tf_op jit(solution)/shard_map/reduce_sum | solution.py:287
  129.7 4.3 %shard_map.177 = bf16[4,112,128]{2,1,0:T(8,128)(2,1)} custom-call(bf16[112,128]{1,0:T(8,128)(2,1)} %reduce_sum.226.refs_0_), custom_call_target="tpu_custom_call" | custom-call | tf_op jit(solution)/shard_map/pallas_call | solution.py:224
  134.0 1.0 convert_element_type.268
  136.0 0.8 copy.151
  136.9 0.8 copy.148
  138.9 0.7 copy.149
  139.7 0.8 copy.150
  (134 shorter events, 11.2 us)
Async XLA Ops:
  0.6 24.1 %copy-start = (bf16[640,896]{1,0:T(8,128)(2,1)S(1)}, bf16[640,896]{1,0:T(8,128)(2,1)}, u32[]{:S(2)}) copy-start(bf16[640,896]{1,0:T(8,128)(2,1)} %param.23) | copy-start | bytes 3440644
  1.7 1.8 %copy-start.4 = (bf16[256,224]{1,0:T(8,128)(2,1)}, bf16[256,224]{1,0:T(8,128)(2,1)S(1)}, u32[]{:S(2)}) copy-start(bf16[256,224]{1,0:T(8,128)(2,1)S(1)} %copy.117.refs_0_) | copy-start | bytes 344068
  2.8 0.8 copy-start.7
  22.6 1.9 %copy-start.13 = (bf16[4,256,224]{2,1,0:T(8,128)(2,1)S(1)}, bf16[4,256,224]{2,1,0:T(8,128)(2,1)}, u32[]{:S(2)}) copy-start(bf16[4,256,224]{2,1,0:T(8,128)(2,1)} %get-tuple-element.25) | copy-start | bytes 1376260
  25.4 3.8 %copy-start.34 = (bf16[2,896,640]{2,1,0:T(8,128)(2,1)S(1)}, bf16[2,896,640]{2,1,0:T(8,128)(2,1)}, u32[]{:S(2)}) copy-start(bf16[2,896,640]{2,1,0:T(8,128)(2,1)} %param.22) | copy-start | bytes 6881284
  28.3 0.9 copy-start.35
  33.4 1.2 copy-start.33
  33.4 1.4 copy-start.19
  34.6 14.8 %copy-start.25 = (bf16[256,224]{0,1:T(8,128)(2,1)S(1)}, bf16[256,224]{0,1:T(8,128)(2,1)}, u32[]{:S(2)}) copy-start(bf16[256,224]{0,1:T(8,128)(2,1)} %param.14) | copy-start | bytes 344068
  34.6 14.9 %copy-start.5 = (bf16[256,224]{1,0:T(8,128)(2,1)S(1)}, bf16[256,224]{1,0:T(8,128)(2,1)}, u32[]{:S(2)}) copy-start(bf16[256,224]{1,0:T(8,128)(2,1)} %copy-done.4) | copy-start | bytes 344068
  36.1 14.7 %copy-start.26 = (bf16[256,224]{0,1:T(8,128)(2,1)S(1)}, bf16[256,224]{0,1:T(8,128)(2,1)}, u32[]{:S(2)}) copy-start(bf16[256,224]{0,1:T(8,128)(2,1)} %param.13) | copy-start | bytes 344068
  48.7 2.2 %copy-start.20 = (f32[256,224]{1,0:T(8,128)S(1)}, f32[256,224]{1,0:T(8,128)}, u32[]{:S(2)}) copy-start(f32[256,224]{1,0:T(8,128)} %get-tuple-element.28) | copy-start | bytes 688132
  49.6 2.1 %copy-start.15 = (bf16[2,224,128]{2,1,0:T(8,128)(2,1)S(1)}, bf16[2,224,128]{2,1,0:T(8,128)(2,1)}, u32[]{:S(2)}) copy-start(bf16[2,224,128]{2,1,0:T(8,128)(2,1)} %param.20) | copy-start | bytes 344068
  87.7 1.3 copy-start.1
  89.0 1.5 %copy-start.8 = (bf16[896,128]{1,0:T(8,128)(2,1)S(1)}, bf16[896,128]{1,0:T(8,128)(2,1)}, u32[]{:S(2)}) copy-start(bf16[896,128]{1,0:T(8,128)(2,1)} %param.19) | copy-start | bytes 688132
  90.5 1.1 copy-start.10
  91.4 2.4 %copy-start.21 = (bf16[256,128]{0,1:T(8,128)(2,1)}, bf16[256,128]{0,1:T(8,128)(2,1)S(1)}, u32[]{:S(2)}) copy-start(bf16[256,128]{0,1:T(8,128)(2,1)S(1)} %get-tuple-element.88) | copy-start | bytes 196612
  91.4 1.1 copy-start.31
  91.4 1.4 %copy-start.32 = (s32[12]{0:T(128)S(1)}, s32[12]{0:T(128)}, u32[]{:S(2)}) copy-start(s32[12]{0:T(128)} %param.17) | copy-start | bytes 148
  92.5 1.7 %copy-start.23 = (bf16[256,128]{0,1:T(8,128)(2,1)}, bf16[256,128]{0,1:T(8,128)(2,1)S(1)}, u32[]{:S(2)}) copy-start(bf16[256,128]{0,1:T(8,128)(2,1)S(1)} %get-tuple-element.86) | copy-start | bytes 196612
  94.0 1.0 copy-start.2
  94.2 0.5 copy-start.30
  98.1 2.1 %copy-start.24 = (bf16[256,128]{0,1:T(8,128)(2,1)S(1)}, bf16[256,128]{0,1:T(8,128)(2,1)}, u32[]{:S(2)}) copy-start(bf16[256,128]{0,1:T(8,128)(2,1)} %copy-done.23) | copy-start | bytes 196612
  100.4 0.8 copy-start.22
  102.0 2.1 %copy-start.14 = (f32[256,128]{0,1:T(8,128)S(1)}, f32[256,128]{0,1:T(8,128)}, u32[]{:S(2)}) copy-start(f32[256,128]{0,1:T(8,128)} %get-tuple-element.87) | copy-start | bytes 393220
  102.0 2.2 %copy-start.12 = (f32[256,128]{0,1:T(8,128)S(1)}, f32[256,128]{0,1:T(8,128)}, u32[]{:S(2)}) copy-start(f32[256,128]{0,1:T(8,128)} %get-tuple-element.89) | copy-start | bytes 393220
  103.1 1.9 %copy-start.11 = (bf16[4,224,128]{2,1,0:T(8,128)(2,1)S(1)}, bf16[4,224,128]{2,1,0:T(8,128)(2,1)}, u32[]{:S(2)}) copy-start(bf16[4,224,128]{2,1,0:T(8,128)(2,1)} %get-tuple-element.33) | copy-start | bytes 688132
  105.4 1.2 copy-start.9
  108.2 27.5 %copy-start.16 = (bf16[8,2,2,16,224]{4,3,2,1,0:T(8,128)(2,1)S(1)}, bf16[8,2,2,16,224]{4,3,2,1,0:T(8,128)(2,1)}, u32[]{:S(2)}) copy-start(bf16[8,2,2,16,224]{4,3,2,1,0:T(8,128)(2,1)} %get-tuple-element.27) | copy-start | bytes 688132
  128.1 7.5 %copy-start.29 = (f32[4,2,128]{2,1,0:T(2,128)S(1)}, f32[4,2,128]{2,1,0:T(2,128)}, u32[]{:S(2)}) copy-start(f32[4,2,128]{2,1,0:T(2,128)} %get-tuple-element.37) | copy-start | bytes 12292
  134.0 1.8 %copy-start.3 = (bf16[1,2,8,16,224]{4,3,2,1,0:T(8,128)(2,1)S(1)}, bf16[1,2,8,16,224]{4,3,2,1,0:T(8,128)(2,1)}, u32[]{:S(2)}) copy-start(bf16[1,2,8,16,224]{4,3,2,1,0:T(8,128)(2,1)} %copy.131) | copy-start | bytes 344068
  134.0 1.8 %copy-start.18 = (f32[256,224]{1,0:T(8,128)S(1)}, f32[256,224]{1,0:T(8,128)}, u32[]{:S(2)}) copy-start(f32[256,224]{1,0:T(8,128)} %get-tuple-element.36) | copy-start | bytes 688132
  135.7 1.0 copy-start.17
  135.8 1.8 %copy-start.28 = (bf16[4,112,128]{2,1,0:T(8,128)(2,1)S(1)}, bf16[4,112,128]{2,1,0:T(8,128)(2,1)}, u32[]{:S(2)}) copy-start(bf16[4,112,128]{2,1,0:T(8,128)(2,1)} %get-tuple-element.40) | copy-start | bytes 344068
  135.8 2.5 %copy-start.27 = (bf16[4,112,128]{2,1,0:T(8,128)(2,1)S(1)}, bf16[4,112,128]{2,1,0:T(8,128)(2,1)}, u32[]{:S(2)}) copy-start(bf16[4,112,128]{2,1,0:T(8,128)(2,1)} %get-tuple-element.38) | copy-start | bytes 344068
  136.0 3.7 %copy-start.6 = (bf16[1,2,8,16,224]{4,3,2,1,0:T(8,128)(2,1)S(1)}, bf16[1,2,8,16,224]{4,3,2,1,0:T(8,128)(2,1)}, u32[]{:S(2)}) copy-start(bf16[1,2,8,16,224]{4,3,2,1,0:T(8,128)(2,1)} %copy.132) | copy-start | bytes 344068
